TPU v7x, 128 devices: a whole 4x4x4 slice. The times are simulated.
128 devices in a mesh: ctx: 8 (over x_lo, z), tp: 16 (over x_hi, y, core).
Axes of the slice: x: 4 (x_hi: 2, x_lo: 2; x = x_hi * 2 + x_lo), y: 4, z: 4, core: 2. Of those that a mesh axis runs over, the one named last changes fastest.
Arguments:
- token_ids: int32 [16384], P('ctx'), may hold values from 0 to 15
- embedding: bfloat16 [16, 2048], P(None, 'tp'), may hold values from -64 to 64
- norm_gain: float32 [2048], P('tp'), may hold values from 0.25 to 1.75
- proj_blocks: bfloat16 [16, 128, 384], P('tp'), may hold values from -0.5 to 0.5
- proj_mixers: bfloat16 [3, 128, 16, 16], P(None, 'tp'), may hold values from -1.5 to 1.5
- out_blocks: bfloat16 [16, 128, 128], P('tp'), may hold values from -0.5 to 0.5
- out_mixers: bfloat16 [128, 16, 16], P('tp'), may hold values from -1.5 to 1.5
- filters: bfloat16 [2048, 16384], P('tp', 'ctx'), may hold values from -2 to 2
- cotangent: bfloat16 [2048, 16384], P('tp', 'ctx'), may hold values from -1 to 1
Outputs:
- layer_out: bfloat16 [2048, 16384], P('tp', 'ctx')
- filter_grad: float32 [2048, 16384], P('tp', 'ctx')
- embed_grad: float32 [16, 2048], P(None, 'tp')
- gain_grad: float32 [2048], P('tp')
All inputs are finite; a program needn't handle non-finite values.
Results may differ from a plain program's by a relative error of at most 0.0097.
Values may be sent and summed in bfloat16 or wider, within the bound.
A program may use at most 64 MiB of HBM per device.

v0:
```python
import math

import jax
import jax.numpy as jnp
import numpy as np
from jax import lax
from jax.sharding import PartitionSpec as P

WIDTH = 2048
EPS = 1e-06
HI = lax.Precision.HIGHEST
SPAN = 32768
BF = jnp.bfloat16
F32 = jnp.float32


def tables():
    idx = np.arange(128)
    half = idx + 0.5
    first = 2 * np.pi * np.outer(half, idx) / 256.0
    c1 = np.concatenate([np.cos(first), -np.sin(first)], 0)
    twist = 2 * np.pi * np.outer(half, idx) / SPAN
    second = 2 * np.pi * (np.outer(idx, idx) % 128) / 128.0
    co, si = np.cos(second), np.sin(second)
    c2 = np.block([[co, -si], [si, co]])
    i1 = np.block([[co, si], [-si, co]])
    i2 = np.concatenate([np.cos(first.T), -np.sin(first.T)], 1) * (2.0 / SPAN)
    to = lambda a, d: jnp.asarray(a, F32).astype(d)
    return to(c1, BF), to(np.cos(twist), F32), to(np.sin(twist), F32), to(c2, BF), to(i1, BF), to(i2, BF)


def dot(formula, a, b):
    return jnp.einsum(formula, a.astype(BF), b.astype(BF), preferred_element_type=F32)


def forward(signal, consts, real_only=False):
    c1, tc, ts, c2, _, _ = consts
    a = dot("kq,cqr->ckr", c1, signal)
    re, im = a[:, :128], a[:, 128:]
    b = jnp.concatenate([re * tc + im * ts, im * tc - re * ts], axis=2)
    return dot("cks,sj->ckj", b, c2[:, :128] if real_only else c2)


def inverse(spectrum, consts):
    _, tc, ts, _, i1, i2 = consts
    u = dot("ckj,js->cks", spectrum, i1[: spectrum.shape[2]])
    re, im = u[:, :, :128], u[:, :, 128:]
    v = jnp.concatenate([re * tc - im * ts, im * tc + re * ts], axis=1)
    return dot("qk,ckr->cqr", i2, v)


def everyone(x, axis, count):
    return lax.all_to_all(jnp.broadcast_to(x[None], (count,) + x.shape), axis, 0, 0, tiled=True)


def local(token_ids, embedding, norm_gain, proj_blocks, proj_mixers, out_blocks, out_mixers, filters, cotangent):
    consts = tables()
    tokens = token_ids.shape[0]
    nctx, ntp = lax.axis_size("ctx"), lax.axis_size("tp")
    back_pieces = jnp.einsum(
        "igm,imt->igt", out_mixers, cotangent.reshape(8, 16, tokens), preferred_element_type=F32
    ).astype(BF)
    filter_parts = lax.all_to_all(filters.reshape(nctx, 16, 16, 128), "ctx", 0, 0, tiled=True)
    filter_whole = filter_parts.transpose(1, 0, 2, 3).reshape(16, 128, 128)
    back_section = lax.all_to_all(back_pieces, "tp", split_axis=1, concat_axis=0, tiled=True)
    grad_branch = jnp.einsum(
        "ji,it->jt", out_blocks[0], back_section.reshape(128, tokens), preferred_element_type=F32
    )
    all_ids = everyone(token_ids, "ctx", nctx).reshape(nctx * tokens)
    ids16 = lax.broadcasted_iota(jnp.int32, (16, tokens), 0)
    one_hot = (token_ids[None, :] == ids16).astype(F32)
    emb = embedding.astype(F32)
    squares = jnp.sum(everyone(jnp.sum(emb * emb, axis=1), "tp", ntp).reshape(ntp, 16), axis=0)
    scaling = lax.rsqrt(squares / WIDTH + EPS)
    normed = (emb * scaling[:, None] * norm_gain[None, :]).astype(BF)
    first = jnp.einsum("vj,jk->kv", normed, proj_blocks[0], preferred_element_type=F32).astype(BF)
    pieces = lax.all_to_all(first.reshape(3, 128, 1, 16), "tp", split_axis=1, concat_axis=2, tiled=True)
    table = jnp.einsum("pigv,pigm->pimv", pieces, proj_mixers, preferred_element_type=F32).reshape(3, 128, 16)
    gated_table = (table[0] * table[1]).astype(BF)
    here = lax.axis_index("ctx")
    mine = lax.dynamic_slice_in_dim(gated_table, here * 16, 16, 0)
    all_hot = (all_ids[None, :] == lax.broadcasted_iota(jnp.int32, (16, nctx * tokens), 0)).astype(BF)
    gated = dot("cv,vt->ct", mine, all_hot).astype(BF).reshape(16, 128, 128)
    gate_outer = jnp.einsum("cv,vt->ct", table[2], one_hot, precision=HI)
    grad_filtered = (grad_branch * gate_outer).astype(BF)
    grad_parts = lax.all_to_all(grad_filtered.reshape(nctx, 16, 16, 128), "ctx", 0, 0, tiled=True)
    grad_whole = grad_parts.transpose(1, 0, 2, 3).reshape(16, 128, 128)
    even = 2.0 * forward(filter_whole, consts, True)
    even2 = jnp.concatenate([even, even], axis=2)
    spec_x = forward(gated, consts)
    filtered_whole = inverse(spec_x * even2, consts).astype(BF)
    filtered = lax.all_to_all(
        filtered_whole.reshape(16, nctx, 16, 128).transpose(1, 0, 2, 3), "ctx", 0, 0, tiled=True
    ).reshape(128, tokens)
    branch = (gate_outer * filtered).astype(BF)
    out_section = jnp.einsum("jt,ji->it", branch, out_blocks[0], preferred_element_type=F32).astype(BF)
    out_pieces = lax.all_to_all(out_section.reshape(128, 1, tokens), "tp", 0, 1, tiled=True)
    mixture = jnp.einsum("igt,igm->imt", out_pieces, out_mixers, preferred_element_type=F32).reshape(128, tokens)
    embedded = jnp.einsum("vc,vt->ct", embedding, one_hot.astype(BF), preferred_element_type=F32)
    layer_out = (embedded + mixture).astype(BF)
    spec_g = forward(grad_whole, consts)
    grad_gated = inverse(spec_g * even2, consts)
    cross = 2.0 * (spec_g[:, :, :128] * spec_x[:, :, :128] + spec_g[:, :, 128:] * spec_x[:, :, 128:])
    kernel_whole = inverse(cross, consts).astype(BF)
    filter_grad = (
        lax.all_to_all(kernel_whole.reshape(16, nctx, 16, 128).transpose(1, 0, 2, 3), "ctx", 0, 0, tiled=True)
        .reshape(128, tokens)
        .astype(F32)
    )
    gg = dot("ct,vt->cv", grad_gated.reshape(16, nctx * tokens), all_hot)
    gp2 = dot("ct,vt->cv", grad_branch * filtered, one_hot)
    ct = dot("ct,vt->cv", cotangent, one_hot)
    gg_all = everyone(gg, "ctx", nctx).reshape(128, 16)
    sums = jnp.sum(everyone(jnp.stack([gp2, ct]), "ctx", nctx).reshape(nctx, 2, 128, 16), axis=0)
    grads = jnp.stack([gg_all * table[1], gg_all * table[0], sums[0]]).reshape(3, 8, 16, 16)
    grad_first = jnp.einsum("pigm,pimv->pigv", proj_mixers.astype(F32), grads, precision=HI)
    grad_first = lax.all_to_all(grad_first, "tp", split_axis=2, concat_axis=1, tiled=True)
    grad_normed = jnp.einsum(
        "jk,kv->vj", proj_blocks[0].astype(F32), grad_first.reshape(384, 16), precision=HI
    )
    gain_grad = jnp.sum(grad_normed * emb * scaling[:, None], axis=0)
    cross_part = jnp.sum(grad_normed * norm_gain[None, :] * emb, axis=1)
    cross_total = jnp.sum(everyone(cross_part, "tp", ntp).reshape(ntp, 16), axis=0)
    embed_grad = (
        sums[1].T
        + scaling[:, None] * norm_gain[None, :] * grad_normed
        - emb * (scaling**3 * cross_total / WIDTH)[:, None]
    )
    return (layer_out, filter_grad, embed_grad, gain_grad)


def solution(mesh):
    in_specs = (
        P("ctx"),
        P(None, "tp"),
        P("tp"),
        P("tp", None, None),
        P(None, "tp", None, None),
        P("tp", None, None),
        P("tp", None, None),
        P("tp", "ctx"),
        P("tp", "ctx"),
    )
    out_specs = (P("tp", "ctx"), P("tp", "ctx"), P(None, "tp"), P("tp"))
    return jax.shard_map(local, mesh=mesh, in_specs=in_specs, out_specs=out_specs, check_vma=False)
```

profile of v0, /device:TPU:1, one launch (start us, length us, event | category | flops | bytes accessed | tf_op | source)
XLA Modules:
  0.0 186.1 jit_solution(10369986576963728010)
XLA Ops:
  1.6 15.2 %all_to_all.114 = f32[16,1,16]{2,1,0:T(1,128)S(1)} all-to-all(f32[16,1,16]{2,1,0:T(1,128)S(1)} %broadcast_in_dim.10), channel_id=1, replica_groups=mesh['ctx'=8,'tp'=16] {'tp'}, dimensions={0} | all-to-all | bytes 2048 | tf_op jit(solution)/shard_map/all_to_all | solution.py:53
  18.8 4.0 %all-to-all-start.1 = ((bf16[16,2,192]{2,1,0:T(2,128)(2,1)}), bf16[16,2,192]{2,1,0:T(2,128)(2,1)S(1)}, u32[]{:S(2)}, u32[]{:S(2)}) async-start(bf16[16,2,192]{2,1,0:T(2,128)(2,1)} %reshape.140), calls=%async_computation.1 | async-start | bytes 32768 | tf_op jit(solution)/shard_map/all_to_all | solution.py:77
  25.0 5.2 %all-to-all-done.1 = bf16[16,2,192]{2,1,0:T(2,128)(2,1)S(1)} async-done(((bf16[16,2,192]{2,1,0:T(2,128)(2,1)}), bf16[16,2,192]{2,1,0:T(2,128)(2,1)S(1)}, u32[]{:S(2)}, u32[]{:S(2)}) %all-to-all-start.1) | async-done | bytes 12320 | tf_op jit(solution)/shard_map/all_to_all | solution.py:77
  30.1 3.8 %all-to-all-start.6 = ((bf16[8,16,2048]{2,0,1:T(8,128)(2,1)}), bf16[8,16,2048]{2,0,1:T(8,128)(2,1)S(1)}, u32[]{:S(2)}, u32[]{:S(2)}) async-start(bf16[8,16,2048]{2,0,1:T(8,128)(2,1)} %copy.240), calls=%async_computation.6 | async-start | bytes 1048576 | tf_op jit(solution)/shard_map/all_to_all | solution.py:65
  36.1 9.2 %all-to-all-done.6 = bf16[8,16,2048]{2,0,1:T(8,128)(2,1)S(1)} async-done(((bf16[8,16,2048]{2,0,1:T(8,128)(2,1)}), bf16[8,16,2048]{2,0,1:T(8,128)(2,1)S(1)}, u32[]{:S(2)}, u32[]{:S(2)}) %all-to-all-start.6) | async-done | bytes 524320 | tf_op jit(solution)/shard_map/all_to_all | solution.py:65
  45.3 5.1 %all-to-all-start.3 = ((bf16[8,16,16,128]{3,2,1,0:T(8,128)(2,1)}), bf16[8,16,16,128]{3,2,1,0:T(8,128)(2,1)S(1)}, u32[]{:S(2)}, u32[]{:S(2)}) async-start(bf16[8,16,16,128]{3,2,1,0:T(8,128)(2,1)} %bitcast.79), calls=%async_computation.3 | async-start | bytes 1048576 | tf_op jit(solution)/shard_map/all_to_all | solution.py:63
  52.7 5.0 %all-to-all-done.3 = bf16[8,16,16,128]{3,2,1,0:T(8,128)(2,1)S(1)} async-done(((bf16[8,16,16,128]{3,2,1,0:T(8,128)(2,1)}), bf16[8,16,16,128]{3,2,1,0:T(8,128)(2,1)S(1)}, u32[]{:S(2)}, u32[]{:S(2)}) %all-to-all-start.3) | async-done | bytes 524320 | tf_op jit(solution)/shard_map/all_to_all | solution.py:63
  57.7 5.2 %all-to-all-start.7 = ((bf16[8,16,16,128]{3,2,1,0:T(8,128)(2,1)}), bf16[8,16,16,128]{3,2,1,0:T(8,128)(2,1)S(1)}, u32[]{:S(2)}, u32[]{:S(2)}) async-start(bf16[8,16,16,128]{3,2,1,0:T(8,128)(2,1)} %bitcast.85), calls=%async_computation.7 | async-start | bytes 1048576 | tf_op jit(solution)/shard_map/all_to_all | solution.py:86
  64.0 1.5 fusion.95
  65.4 4.7 %all-to-all-done.7 = bf16[8,16,16,128]{3,2,1,0:T(8,128)(2,1)S(1)} async-done(((bf16[8,16,16,128]{3,2,1,0:T(8,128)(2,1)}), bf16[8,16,16,128]{3,2,1,0:T(8,128)(2,1)S(1)}, u32[]{:S(2)}, u32[]{:S(2)}) %all-to-all-start.7) | async-done | bytes 524320 | tf_op jit(solution)/shard_map/all_to_all | solution.py:86
  70.8 5.2 %all-to-all-start.2 = ((s32[8,1,2048]{2,1,0:T(1,128)}), s32[8,1,2048]{2,1,0:T(1,128)S(1)}, u32[]{:S(2)}, u32[]{:S(2)}) async-start(s32[8,1,2048]{2,1,0:T(1,128)} %broadcast_in_dim.11), calls=%async_computation.2 | async-start | bytes 131072 | tf_op jit(solution)/shard_map/all_to_all | solution.py:53
  76.0 1.3 convolution_bitcast_fusion.2
  81.1 1.2 fusion.8
  82.4 1.3 copy.251
  84.9 5.1 %all-to-all-start.10 = ((f32[8,1,256]{2,1,0:T(1,128)}), f32[8,1,256]{2,1,0:T(1,128)S(1)}, u32[]{:S(2)}, u32[]{:S(2)}) async-start(f32[8,1,256]{2,1,0:T(1,128)} %reshape.144), calls=%async_computation.10 | async-start | bytes 16384 | tf_op jit(solution)/shard_map/all_to_all | solution.py:53
  90.0 5.0 %all-to-all-done.10 = f32[8,1,256]{2,1,0:T(1,128)S(1)} async-done(((f32[8,1,256]{2,1,0:T(1,128)}), f32[8,1,256]{2,1,0:T(1,128)S(1)}, u32[]{:S(2)}, u32[]{:S(2)}) %all-to-all-start.10) | async-done | bytes 8224 | tf_op jit(solution)/shard_map/all_to_all | solution.py:53
  100.4 1.6 subtract_convert_fusion.1
  103.3 3.7 %all-to-all-start.4 = ((bf16[8,16,16,128]{3,2,1,0:T(8,128)(2,1)}), bf16[8,16,16,128]{3,2,1,0:T(8,128)(2,1)S(1)}, u32[]{:S(2)}, u32[]{:S(2)}) async-start(bf16[8,16,16,128]{3,2,1,0:T(8,128)(2,1)} %bitcast.191), calls=%async_computation.4 | async-start | bytes 1048576 | tf_op jit(solution)/shard_map/all_to_all | solution.py:92
  107.2 6.6 %all-to-all-done.4 = bf16[8,16,16,128]{3,2,1,0:T(8,128)(2,1)S(1)} async-done(((bf16[8,16,16,128]{3,2,1,0:T(8,128)(2,1)}), bf16[8,16,16,128]{3,2,1,0:T(8,128)(2,1)S(1)}, u32[]{:S(2)}, u32[]{:S(2)}) %all-to-all-start.4) | async-done | bytes 524320 | tf_op jit(solution)/shard_map/all_to_all | solution.py:92
  114.5 8.4 %all_to_all.115 = f32[8,2,128,16]{2,3,1,0:T(8,128)S(1)} all-to-all(f32[8,2,128,16]{2,3,1,0:T(8,128)S(1)} %broadcast_in_dim.12), channel_id=1, replica_groups=mesh['ctx'=8,'tp'=16] {'ctx'}, dimensions={0} | all-to-all | bytes 262144 | tf_op jit(solution)/shard_map/all_to_all | solution.py:53
  124.2 9.7 %all-to-all-start.11 = ((f32[16,1,384]{2,1,0:T(1,128)}), f32[16,1,384]{2,1,0:T(1,128)S(1)}, u32[]{:S(2)}, u32[]{:S(2)}) async-start(f32[16,1,384]{2,1,0:T(1,128)} %reshape.146), calls=%async_computation.11 | async-start | bytes 49152 | tf_op jit(solution)/shard_map/all_to_all | solution.py:117
  133.9 1.5 convolution_convert_fusion.4
  136.3 4.7 %all-to-all-done.11 = f32[16,1,384]{2,1,0:T(1,128)S(1)} async-done(((f32[16,1,384]{2,1,0:T(1,128)}), f32[16,1,384]{2,1,0:T(1,128)S(1)}, u32[]{:S(2)}, u32[]{:S(2)}) %all-to-all-start.11) | async-done | bytes 24608 | tf_op jit(solution)/shard_map/all_to_all | solution.py:117
  141.1 3.5 %all-to-all-start.8 = ((bf16[8,16,16,128]{3,2,1,0:T(8,128)(2,1)}), bf16[8,16,16,128]{3,2,1,0:T(8,128)(2,1)S(1)}, u32[]{:S(2)}, u32[]{:S(2)}) async-start(bf16[8,16,16,128]{3,2,1,0:T(8,128)(2,1)} %bitcast.198), calls=%async_computation.8 | async-start | bytes 1048576 | tf_op jit(solution)/shard_map/all_to_all | solution.py:106
  146.5 6.5 %all-to-all-done.8 = bf16[8,16,16,128]{3,2,1,0:T(8,128)(2,1)S(1)} async-done(((bf16[8,16,16,128]{3,2,1,0:T(8,128)(2,1)}), bf16[8,16,16,128]{3,2,1,0:T(8,128)(2,1)S(1)}, u32[]{:S(2)}, u32[]{:S(2)}) %all-to-all-start.8) | async-done | bytes 524320 | tf_op jit(solution)/shard_map/all_to_all | solution.py:106
  153.6 5.2 %all-to-all-start.12 = ((f32[16,1,16]{2,1,0:T(1,128)}), f32[16,1,16]{2,1,0:T(1,128)S(1)}, u32[]{:S(2)}, u32[]{:S(2)}) async-start(f32[16,1,16]{2,1,0:T(1,128)} %broadcast_in_dim.14), calls=%async_computation.12 | async-start | bytes 16384 | tf_op jit(solution)/shard_map/all_to_all | solution.py:53
  158.8 1.4 fusion.2
  160.7 2.1 %reduce.3 = bf16[128,2048]{0,1:T(8,128)(2,1)S(1)} reduce(bf16[128,1,2048]{0,2,1:T(8,128)(2,1)} %fusion.2, bf16[]{:T(256)} %broadcast.60), dimensions={1}, to_apply=%copy.236.reduce_sub_computation | reduce | bytes 1048578 | tf_op jit(solution)/shard_map/reshape | solution.py:97
  163.0 1.3 reshape.142
  164.3 1.4 all-to-all-done.12
  165.7 5.9 %all-to-all-start.5 = ((bf16[16,2,8192]{2,1,0:T(2,128)(2,1)}), bf16[16,2,8192]{2,1,0:T(2,128)(2,1)S(1)}, u32[]{:S(2)}, u32[]{:S(2)}) async-start(bf16[16,2,8192]{2,1,0:T(2,128)(2,1)} %reshape.142), calls=%async_computation.5 | async-start | bytes 1048576 | tf_op jit(solution)/shard_map/all_to_all | solution.py:97
  173.4 9.5 %all-to-all-done.5 = bf16[16,2,8192]{2,1,0:T(2,128)(2,1)S(1)} async-done(((bf16[16,2,8192]{2,1,0:T(2,128)(2,1)}), bf16[16,2,8192]{2,1,0:T(2,128)(2,1)S(1)}, u32[]{:S(2)}, u32[]{:S(2)}) %all-to-all-start.5) | async-done | bytes 524320 | tf_op jit(solution)/shard_map/all_to_all | solution.py:97
  (144 shorter events, 33.8 us)
Async XLA Ops:
  0.6 22.2 %copy-start = (bf16[128,2048]{1,0:T(8,128)(2,1)S(1)}, bf16[128,2048]{1,0:T(8,128)(2,1)}, u32[]{:S(2)}) copy-start(bf16[128,2048]{1,0:T(8,128)(2,1)} %param.23) | copy-start | bytes 1572868
  0.6 33.3 %copy-start.12 = (bf16[128,2048]{1,0:T(8,128)(2,1)S(1)}, bf16[128,2048]{1,0:T(8,128)(2,1)}, u32[]{:S(2)}) copy-start(bf16[128,2048]{1,0:T(8,128)(2,1)} %param.22) | copy-start | bytes 1572868
  18.8 11.3 %all-to-all-start.1 = ((bf16[16,2,192]{2,1,0:T(2,128)(2,1)}), bf16[16,2,192]{2,1,0:T(2,128)(2,1)S(1)}, u32[]{:S(2)}, u32[]{:S(2)}) async-start(bf16[16,2,192]{2,1,0:T(2,128)(2,1)} %reshape.140), calls=%async_computation.1 | async-start | bytes 32768 | tf_op jit(solution)/shard_map/all_to_all | solution.py:77
  22.8 12.4 %copy-start.15 = (bf16[3,8,16,16]{3,2,1,0:T(8,128)(2,1)S(1)}, bf16[3,8,16,16]{3,2,1,0:T(8,128)(2,1)}, u32[]{:S(2)}) copy-start(bf16[3,8,16,16]{3,2,1,0:T(8,128)(2,1)} %param.19) | copy-start | bytes 36868
  23.9 11.6 %copy-start.18 = (s32[2048]{0:T(1024)S(1)}, s32[2048]{0:T(1024)}, u32[]{:S(2)}) copy-start(s32[2048]{0:T(1024)} %param.15) | copy-start | bytes 24580
  30.1 15.1 %all-to-all-start.6 = ((bf16[8,16,2048]{2,0,1:T(8,128)(2,1)}), bf16[8,16,2048]{2,0,1:T(8,128)(2,1)S(1)}, u32[]{:S(2)}, u32[]{:S(2)}) async-start(bf16[8,16,2048]{2,0,1:T(8,128)(2,1)} %copy.240), calls=%async_computation.6 | async-start | bytes 1048576 | tf_op jit(solution)/shard_map/all_to_all | solution.py:65
  33.9 16.4 %copy-start.20 = (bf16[1,128,128]{2,1,0:T(8,128)(2,1)S(1)}, bf16[1,128,128]{2,1,0:T(8,128)(2,1)}, u32[]{:S(2)}) copy-start(bf16[1,128,128]{2,1,0:T(8,128)(2,1)} %param.20) | copy-start | bytes 98308
  36.1 15.7 %copy-start.3 = (f32[128,2048]{1,0:T(8,128)}, f32[128,2048]{1,0:T(8,128)S(1)}, u32[]{:S(2)}) copy-start(f32[128,2048]{1,0:T(8,128)S(1)} %fusion.59) | copy-start | bytes 3145732
  45.3 12.4 %all-to-all-start.3 = ((bf16[8,16,16,128]{3,2,1,0:T(8,128)(2,1)}), bf16[8,16,16,128]{3,2,1,0:T(8,128)(2,1)S(1)}, u32[]{:S(2)}, u32[]{:S(2)}) async-start(bf16[8,16,16,128]{3,2,1,0:T(8,128)(2,1)} %bitcast.79), calls=%async_computation.3 | async-start | bytes 1048576 | tf_op jit(solution)/shard_map/all_to_all | solution.py:63
  51.8 12.2 %copy-start.27 = (bf16[256,128]{1,0:T(8,128)(2,1)S(1)}, bf16[256,128]{1,0:T(8,128)(2,1)}, u32[]{:S(2)}) copy-start(bf16[256,128]{1,0:T(8,128)(2,1)} %constant.44) | copy-start | bytes 196612
  57.7 12.4 %all-to-all-start.7 = ((bf16[8,16,16,128]{3,2,1,0:T(8,128)(2,1)}), bf16[8,16,16,128]{3,2,1,0:T(8,128)(2,1)S(1)}, u32[]{:S(2)}, u32[]{:S(2)}) async-start(bf16[8,16,16,128]{3,2,1,0:T(8,128)(2,1)} %bitcast.85), calls=%async_computation.7 | async-start | bytes 1048576 | tf_op jit(solution)/shard_map/all_to_all | solution.py:86
  65.4 11.9 %copy-start.7 = (f32[128,128]{0,1:T(8,128)S(1)}, f32[128,128]{0,1:T(8,128)}, u32[]{:S(2)}) copy-start(f32[128,128]{0,1:T(8,128)} %constant.36.clone) | copy-start | bytes 196612
  65.4 11.9 %copy-start.8 = (f32[128,128]{0,1:T(8,128)S(1)}, f32[128,128]{0,1:T(8,128)}, u32[]{:S(2)}) copy-start(f32[128,128]{0,1:T(8,128)} %constant.35.clone) | copy-start | bytes 196612
  70.8 12.9 %all-to-all-start.2 = ((s32[8,1,2048]{2,1,0:T(1,128)}), s32[8,1,2048]{2,1,0:T(1,128)S(1)}, u32[]{:S(2)}, u32[]{:S(2)}) async-start(s32[8,1,2048]{2,1,0:T(1,128)} %broadcast_in_dim.11), calls=%async_computation.2 | async-start | bytes 131072 | tf_op jit(solution)/shard_map/all_to_all | solution.py:53
  84.2 12.8 %copy-start.17 = (bf16[256,128,1]{1,0,2:T(8,128)(2,1)S(1)}, bf16[256,128,1]{1,0,2:T(8,128)(2,1)}, u32[]{:S(2)}) copy-start(bf16[256,128,1]{1,0,2:T(8,128)(2,1)} %constant.50) | copy-start | bytes 196612
  84.9 10.2 %all-to-all-start.10 = ((f32[8,1,256]{2,1,0:T(1,128)}), f32[8,1,256]{2,1,0:T(1,128)S(1)}, u32[]{:S(2)}, u32[]{:S(2)}) async-start(f32[8,1,256]{2,1,0:T(1,128)} %reshape.144), calls=%async_computation.10 | async-start | bytes 16384 | tf_op jit(solution)/shard_map/all_to_all | solution.py:53
  100.4 1.6 copy-start.30
  102.4 11.5 %copy-start.2 = (f32[128,2048]{1,0:T(8,128)S(1)}, f32[128,2048]{1,0:T(8,128)}, u32[]{:S(2)}) copy-start(f32[128,2048]{1,0:T(8,128)} %copy-done.1) | copy-start | bytes 3145732
  103.3 10.6 %all-to-all-start.4 = ((bf16[8,16,16,128]{3,2,1,0:T(8,128)(2,1)}), bf16[8,16,16,128]{3,2,1,0:T(8,128)(2,1)S(1)}, u32[]{:S(2)}, u32[]{:S(2)}) async-start(bf16[8,16,16,128]{3,2,1,0:T(8,128)(2,1)} %bitcast.191), calls=%async_computation.4 | async-start | bytes 1048576 | tf_op jit(solution)/shard_map/all_to_all | solution.py:92
  113.8 9.2 %copy-start.16 = (bf16[3,8,16,16]{3,2,1,0:T(8,128)(2,1)S(1)}, bf16[3,8,16,16]{3,2,1,0:T(8,128)(2,1)}, u32[]{:S(2)}) copy-start(bf16[3,8,16,16]{3,2,1,0:T(8,128)(2,1)} %param.19) | copy-start | bytes 36868
  114.0 20.0 %copy-start.9 = (bf16[16,128,128]{1,2,0:T(8,128)(2,1)S(1)}, bf16[16,128,128]{1,2,0:T(8,128)(2,1)}, u32[]{:S(2)}) copy-start(bf16[16,128,128]{1,2,0:T(8,128)(2,1)} %get-tuple-element.36) | copy-start | bytes 1572868
  124.2 16.9 %all-to-all-start.11 = ((f32[16,1,384]{2,1,0:T(1,128)}), f32[16,1,384]{2,1,0:T(1,128)S(1)}, u32[]{:S(2)}, u32[]{:S(2)}) async-start(f32[16,1,384]{2,1,0:T(1,128)} %reshape.146), calls=%async_computation.11 | async-start | bytes 49152 | tf_op jit(solution)/shard_map/all_to_all | solution.py:117
  135.5 10.0 %copy-start.22 = (bf16[1,128,384]{2,1,0:T(8,128)(2,1)S(1)}, bf16[1,128,384]{2,1,0:T(8,128)(2,1)}, u32[]{:S(2)}) copy-start(bf16[1,128,384]{2,1,0:T(8,128)(2,1)} %param.18) | copy-start | bytes 294916
  135.5 10.0 %copy-start.24 = (bf16[16,128]{1,0:T(8,128)(2,1)S(1)}, bf16[16,128]{1,0:T(8,128)(2,1)}, u32[]{:S(2)}) copy-start(bf16[16,128]{1,0:T(8,128)(2,1)} %param.16) | copy-start | bytes 12292
  135.5 10.0 %copy-start.28 = (f32[128]{0:T(128)S(1)}, f32[128]{0:T(128)}, u32[]{:S(2)}) copy-start(f32[128]{0:T(128)} %param.17) | copy-start | bytes 1540
  135.5 23.3 %copy-start.4 = (f32[128,2048]{1,0:T(8,128)S(1)}, f32[128,2048]{1,0:T(8,128)}, u32[]{:S(2)}) copy-start(f32[128,2048]{1,0:T(8,128)} %copy-done.3) | copy-start | bytes 3145732
  135.5 23.3 %copy-start.21 = (bf16[1,128,128]{2,1,0:T(8,128)(2,1)S(1)}, bf16[1,128,128]{2,1,0:T(8,128)(2,1)}, u32[]{:S(2)}) copy-start(bf16[1,128,128]{2,1,0:T(8,128)(2,1)} %param.20) | copy-start | bytes 98308
  141.1 11.9 %all-to-all-start.8 = ((bf16[8,16,16,128]{3,2,1,0:T(8,128)(2,1)}), bf16[8,16,16,128]{3,2,1,0:T(8,128)(2,1)S(1)}, u32[]{:S(2)}, u32[]{:S(2)}) async-start(bf16[8,16,16,128]{3,2,1,0:T(8,128)(2,1)} %bitcast.198), calls=%async_computation.8 | async-start | bytes 1048576 | tf_op jit(solution)/shard_map/all_to_all | solution.py:106
  153.6 12.2 %all-to-all-start.12 = ((f32[16,1,16]{2,1,0:T(1,128)}), f32[16,1,16]{2,1,0:T(1,128)S(1)}, u32[]{:S(2)}, u32[]{:S(2)}) async-start(f32[16,1,16]{2,1,0:T(1,128)} %broadcast_in_dim.14), calls=%async_computation.12 | async-start | bytes 16384 | tf_op jit(solution)/shard_map/all_to_all | solution.py:53
  163.0 9.8 %copy-start.26 = (f32[2,128,16]{1,2,0:T(8,128)S(1)}, f32[2,128,16]{1,2,0:T(8,128)}, u32[]{:S(2)}) copy-start(f32[2,128,16]{1,2,0:T(8,128)} %copy-done.25) | copy-start | bytes 49156
  165.7 17.2 %all-to-all-start.5 = ((bf16[16,2,8192]{2,1,0:T(2,128)(2,1)}), bf16[16,2,8192]{2,1,0:T(2,128)(2,1)S(1)}, u32[]{:S(2)}, u32[]{:S(2)}) async-start(bf16[16,2,8192]{2,1,0:T(2,128)(2,1)} %reshape.142), calls=%async_computation.5 | async-start | bytes 1048576 | tf_op jit(solution)/shard_map/all_to_all | solution.py:97
  171.6 12.1 %copy-start.19 = (bf16[8,16,16]{2,1,0:T(8,128)(2,1)S(1)}, bf16[8,16,16]{2,1,0:T(8,128)(2,1)}, u32[]{:S(2)}) copy-start(bf16[8,16,16]{2,1,0:T(8,128)(2,1)} %param.21) | copy-start | bytes 12292
  (11 other events, 11.1 us)
where the time goes:
time: 188 us; the launch traced here: 186 us
  waiting for transfers between devices  57.9 us (31%)
  starting transfers between devices  56.2 us (30%)
  blocking collectives  23.7 us (13%)
  local copies, waits for them, and re-layouts  21 us (11%)
  matrix products  17.9 us (10%)
  other arithmetic  8.06 us (4%)
    all_to_all x2, blocking collectives, everyone(): lax.all_to_all(jnp.broadcast_to(x[None], (count,) + x.shape), axis, 0, 0,...  23.7 us
    all_to_all x3, starting transfers between devices, everyone(): lax.all_to_all(jnp.broadcast_to(x[None], (count,) + x.shape), axis, 0, 0,...  15.5 us
    unnamed x80, local copies, waits for them, and re-layouts  12.4 us
    all_to_all x1, starting transfers between devices, local(): lax.all_to_all(grad_first, 'tp', split_axis=2, concat_axis=1, tiled=True)  9.73 us
    dot_general x15, matrix products, dot(): jnp.einsum(formula, a.astype(BF), b.astype(BF), preferred_element_type=F32)  9.51 us
    all_to_all x1, waiting for transfers between devices, local(): lax.all_to_all(out_section.reshape(128, 1, tokens), 'tp', 0, 1, tiled=True)  9.5 us
    all_to_all x1, waiting for transfers between devices, local(): lax.all_to_all(back_pieces, 'tp', split_axis=1, concat_axis=0, tiled=True)  9.17 us
    all_to_all x1, waiting for transfers between devices, local(): lax.all_to_all(filtered_whole.reshape(16, nctx, 16, 128).transpose(1, 0,...  6.64 us
  transfers between devices with their start and end apart: 11, of which 10 were waited for; matrix products, arithmetic and copies ran while one was open for 14% of the time, Pallas kernels for 0%

commit v1 on v0

v1 whole, which is shorter than its diff:
```python
import jax
import jax.numpy as jnp
import numpy as np
from jax import lax
from jax.experimental import pallas as pl
from jax.experimental.pallas import tpu as pltpu
from jax.sharding import PartitionSpec as P

WIDTH = 2048
EPS = 1e-06
SPAN = 32768
NC = 8
NT = 16
BF = jnp.bfloat16
F32 = jnp.float32
MESH = pl.DeviceIdType.MESH

FILT_IN, TOK, GF, FILT, FG, GG, SEG = range(7)
BACK, SS, TAB, OUT, GT, CR = range(6)


def dft_tables():
    idx = np.arange(128)
    half = idx + 0.5
    first = 2 * np.pi * np.outer(half, idx) / 256.0
    c1 = np.concatenate([np.cos(first), -np.sin(first)], 0)
    twist = 2 * np.pi * np.outer(half, idx) / SPAN
    second = 2 * np.pi * (np.outer(idx, idx) % 128) / 128.0
    co, si = np.cos(second), np.sin(second)
    c2 = np.block([[co, -si], [si, co]])
    i1 = np.block([[co, si], [-si, co]])
    i2 = np.concatenate([np.cos(first.T), -np.sin(first.T)], 1) * (2.0 / SPAN)
    cast = lambda a, d: jnp.asarray(a, F32).astype(d)
    return (
        cast(c1, BF),
        cast(np.cos(twist), F32),
        cast(np.sin(twist), F32),
        cast(c2, BF),
        cast(i1, BF),
        cast(i2, BF),
    )


def mm(a, b):
    return jnp.dot(a, b, preferred_element_type=F32)


def mm_tn(a, b):
    return lax.dot_general(a, b, (((0,), (0,)), ((), ())), preferred_element_type=F32)


def mm_nt(a, b):
    return lax.dot_general(a, b, (((1,), (1,)), ((), ())), preferred_element_type=F32)


def iota2(rows, lanes):
    return (
        lax.broadcasted_iota(jnp.int32, (rows, lanes), 0),
        lax.broadcasted_iota(jnp.int32, (rows, lanes), 1),
    )


def ones_at(cond):
    return jnp.where(cond, 1.0, 0.0).astype(F32)


def split(x):
    hi = x.astype(BF)
    return hi, (x - hi.astype(F32)).astype(BF)


def kernel(
    tok_ref, emb_ref, gain_ref, blk_ref, mix_ref, oblk_ref, omix_ref, filt_ref, cot_ref,
    c1_ref, tc_ref, ts_ref, c2_ref, i1_ref, i2_ref,
    lay_ref, fgrad_ref, egrad_ref, ggrad_ref,
    r_filt, r_tok, s_gf, r_gf, s_fl, r_fl, s_fg, r_fg, s_gg, r_gg, s_seg, r_seg,
    s_back, r_back, s_ss, r_ss, s_tab, r_tab, s_out, r_out, s_gt, r_gt, s_cr, r_cr,
    w_back, w_two, r_mix, hot, tall, gated_t, grid_a, grid_b, spec_x, spec_s, outer, gbranch,
    ssem_c, rsem_c, ssem_t, rsem_t,
):
    a = lax.axis_index("ctx")
    b = lax.axis_index("tp")

    class Exchange:
        def __init__(self, axis, msg, src, dst):
            self.me, self.n = (a, NC) if axis == "ctx" else (b, NT)
            sends, recvs = (ssem_c, rsem_c) if axis == "ctx" else (ssem_t, rsem_t)

            def copy(k):
                peer = lax.rem(self.me + k, self.n)
                return pltpu.make_async_remote_copy(
                    src_ref=src(peer),
                    dst_ref=dst(self.me),
                    send_sem=sends.at[msg, k],
                    recv_sem=recvs.at[msg, k],
                    device_id={axis: peer},
                    device_id_type=MESH,
                )

            self.copy = copy

        def each(self, act):
            def body(k, carry):
                act(self.copy(k))
                return carry

            lax.fori_loop(1, self.n, body, 0)

        def start(self):
            self.each(lambda c: c.start())

        def recv(self):
            self.each(lambda c: c.wait_recv())

        def drain(self):
            self.each(lambda c: c.wait_send())

    rows16 = lambda ref: (lambda p: ref.at[pl.ds(pl.multiple_of(p * 16, 16), 16), :])
    slot = lambda ref: (lambda p: ref.at[p])
    whole = lambda ref: (lambda p: ref)

    x_filt = Exchange("ctx", FILT_IN, rows16(filt_ref), slot(r_filt))
    x_tok = Exchange("ctx", TOK, whole(tok_ref), slot(r_tok))
    x_gf = Exchange("ctx", GF, slot(s_gf), slot(r_gf))
    x_fl = Exchange("ctx", FILT, slot(s_fl), slot(r_fl))
    x_fg = Exchange("ctx", FG, slot(s_fg), slot(r_fg))
    x_gg = Exchange("ctx", GG, whole(s_gg), slot(r_gg))
    x_seg = Exchange("ctx", SEG, whole(s_seg), slot(r_seg))
    x_back = Exchange("tp", BACK, slot(s_back), slot(r_back))
    x_ss = Exchange("tp", SS, whole(s_ss), slot(r_ss))
    x_tab = Exchange("tp", TAB, slot(s_tab), slot(r_tab))
    x_out = Exchange("tp", OUT, slot(s_out), slot(r_out))
    x_gt = Exchange("tp", GT, slot(s_gt), slot(r_gt))
    x_cr = Exchange("tp", CR, whole(s_cr), slot(r_cr))

    barrier = pltpu.get_barrier_semaphore()

    def greet(axis, me, n):
        def body(k, carry):
            pl.semaphore_signal(
                barrier, inc=1, device_id={axis: lax.rem(me + k, n)}, device_id_type=MESH
            )
            return carry

        lax.fori_loop(1, n, body, 0)

    greet("ctx", a, NC)
    greet("tp", b, NT)

    row128, lane128 = iota2(128, 128)
    p_lane = lane128 >> 4

    row16, lane16 = iota2(16, 128)
    spread = ones_at(((lane16 & 15) == row16) & (lane16 < 48)).astype(BF)
    emb_t = mm_tn(emb_ref[...], spread)
    s_ss[...] = jnp.broadcast_to(jnp.sum(emb_t * emb_t, axis=0, keepdims=True), (8, 128))

    pl.semaphore_wait(barrier, NC - 1 + NT - 1)
    x_ss.start()
    x_tok.start()
    x_filt.start()
    r_ss[b] = s_ss[...]
    r_tok[a] = tok_ref[...]

    tile_m = ones_at((lane16 & 15) == row16).astype(BF)
    row, lane = iota2(256, 128)
    sel_row = ones_at(((row & 7) == (lane >> 4)) & ((row >> 4) == (lane & 15))).astype(BF)
    wide = mm(sel_row, mm(omix_ref[...], tile_m).astype(BF))
    row, lane = iota2(256, 256)
    keep = ((row & 7) == ((lane >> 4) & 7)) & (((row >> 3) & 1) == (lane >> 7))
    w_back[...] = jnp.where(keep, jnp.concatenate([wide, wide], axis=1), 0.0).astype(BF)
    cot2 = jnp.concatenate([cot_ref[:, :1024], cot_ref[:, 1024:]], axis=0)
    s_back[...] = mm(w_back[...], cot2).astype(BF).reshape(NT, 16, 1024)
    x_back.start()
    r_back[b] = s_back[b]
    r_filt[a] = filt_ref[pl.ds(pl.multiple_of(a * 16, 16), 16), :]

    sel_p = ones_at(((row128 & 7) == p_lane) & ((row128 >> 3) == (lane128 & 15))).astype(BF)
    for p in range(3):
        wide = mm(sel_p, mm(mix_ref[p * 128 : (p + 1) * 128, :], tile_m).astype(BF))
        r_mix[p] = jnp.where((row128 & 7) == p_lane, wide, 0.0).astype(BF)
    gain_row = gain_ref[...]
    gain_col = jnp.sum(jnp.where(row128 == lane128, gain_row, 0.0), axis=1, keepdims=True)

    x_ss.recv()
    total = jnp.sum(r_ss[...], axis=0)[0:1, :]
    scal_row = lax.rsqrt(total * (1.0 / WIDTH) + EPS)
    normed = emb_t * scal_row * gain_col
    first = jnp.zeros((128, 128), F32)
    for p in range(3):
        first += mm_tn(
            blk_ref[:, p * 128 : (p + 1) * 128], jnp.where(p_lane == p, normed, 0.0).astype(BF)
        )
    s_tab[...] = first.astype(BF).astype(F32).reshape(NT, 8, 128)
    x_tab.start()
    r_tab[b] = s_tab[b]

    row, lane = iota2(128, 256)
    sel_col = ones_at(((lane >> 4) * 8 + (lane & 7)) == row).astype(BF)
    wide = mm(oblk_ref[...], sel_col)
    low = ((lane >> 3) & 1) == 0
    w_two[...] = jnp.concatenate(
        [jnp.where(low, wide, 0.0), jnp.where(low, 0.0, wide)], axis=0
    ).astype(BF)

    x_tok.recv()
    for src in range(NC):
        ids = r_tok[src]
        for q in range(16):
            hot[src, :, q * 128 : (q + 1) * 128] = ones_at(
                jnp.broadcast_to(ids[q : q + 1, :], (16, 128)) == row16
            ).astype(BF)

    x_tab.recv()
    pieces = r_tab[...].reshape(128, 128)
    table = jnp.zeros((128, 128), F32)
    for p in range(3):
        table += mm_tn(r_mix[p], jnp.where(p_lane == p, pieces, 0.0).astype(BF))
    tall[...] = table
    gated_t[...] = table * pltpu.roll(table, 112, 1)
    outer_hi, outer_lo = split(pltpu.roll(table, 96, 1)[:, :16])
    outer_w = jnp.concatenate([outer_hi, outer_lo], axis=1)
    for h in range(2):
        hot_h = hot[a, :, h * 1024 : (h + 1) * 1024]
        outer[h * 128 : (h + 1) * 128, :] = mm(outer_w, jnp.concatenate([hot_h, hot_h], axis=0))

    x_back.recv()
    gbranch[...] = mm(w_two[...], r_back[...].reshape(256, 1024))
    for h in range(2):
        for s in range(8):
            part = slice(s * 128, (s + 1) * 128)
            hrow = slice(h * 128, (h + 1) * 128)
            grid_a[pl.ds(h * 8 + s, 128, stride=16), :] = gbranch[hrow, part] * outer[hrow, part]
    s_gf[...] = grid_a[...].astype(BF).reshape(NC, 16, 16, 128)
    x_gf.start()
    r_gf[a] = s_gf[a]

    mine = gated_t[pl.ds(pl.multiple_of(a * 16, 16), 16), :][:, :16].astype(BF)
    for src in range(NC):
        vals = mm(mine, hot[src])
        for q in range(16):
            grid_a[pl.ds(src * 16 + q, 16, stride=128), :] = vals[:, q * 128 : (q + 1) * 128]

    tc = tc_ref[...]
    ts = ts_ref[...]

    def forward(signal, second):
        first_stage = mm(c1_ref[...], signal)
        re, im = first_stage[:128], first_stage[128:]
        turned = jnp.concatenate([re * tc + im * ts, im * tc - re * ts], axis=1)
        return mm(turned.astype(BF), second)

    def inverse(spectrum, weights):
        back = mm(spectrum.astype(BF), weights)
        re, im = back[:, :128], back[:, 128:]
        turned = jnp.concatenate([re * tc - im * ts, im * tc + re * ts], axis=0)
        return mm(i2_ref[...], turned.astype(BF))

    def channels(step, body):
        def block(n, carry):
            for u in range(step):
                body(n * step + u)
            return carry

        lax.fori_loop(0, 16 // step, block, 0)

    def at_rows(ref, c):
        return ref.at[pl.ds(pl.multiple_of(c * 128, 128), 128), :]

    def gated_spectrum(c):
        spec_x[c] = forward(at_rows(grid_a, c)[...].astype(BF), c2_ref[...])

    channels(4, gated_spectrum)

    x_filt.recv()
    for src in range(NC):
        for q in range(16):
            grid_b[pl.ds(src * 16 + q, 16, stride=128), :] = r_filt[
                src, :, q * 128 : (q + 1) * 128
            ].astype(F32)

    def filtered_channel(c):
        even = 2.0 * forward(at_rows(grid_b, c)[...].astype(BF), c2_ref[:, :128])
        spec_s[c] = even
        spectrum = spec_x[c] * jnp.concatenate([even, even], axis=1)
        s_fl[:, c] = inverse(spectrum, i1_ref[...]).astype(BF).reshape(NC, 16, 128)

    channels(4, filtered_channel)
    x_fl.start()
    r_fl[a] = s_fl[a]

    x_gf.recv()

    def grad_channel(c):
        spec_g = forward(r_gf[:, c].reshape(128, 128), c2_ref[...])
        even = spec_s[c]
        prod = spec_g * spec_x[c]
        cross = 2.0 * (prod[:, :128] + prod[:, 128:])
        s_fg[:, c] = inverse(cross, i1_ref[:128, :]).astype(BF).reshape(NC, 16, 128)
        at_rows(grid_b, c)[...] = inverse(
            spec_g * jnp.concatenate([even, even], axis=1), i1_ref[...]
        )

    channels(2, grad_channel)
    x_fg.start()
    r_fg[a] = s_fg[a]

    sums = jnp.zeros((16, 32), F32)
    for src in range(NC):
        vals = jnp.concatenate(
            [grid_b[pl.ds(src * 16 + q, 16, stride=128), :] for q in range(16)], axis=1
        ).astype(BF)
        hot_s = hot[src]
        sums += mm_nt(vals, jnp.concatenate([hot_s, hot_s], axis=0))
    s_gg[...] = jnp.concatenate([sums, jnp.zeros((16, 96), F32)], axis=1)
    x_gg.start()
    r_gg[a] = s_gg[...]

    x_fl.recv()
    grid_a[...] = r_fl[...].reshape(2048, 128).astype(F32)
    gp2 = jnp.zeros((16, 128), F32)
    ctt = jnp.zeros((16, 128), F32)
    branch = []
    for h in range(2):
        hrow = slice(h * 128, (h + 1) * 128)
        filtered = jnp.concatenate(
            [grid_a[pl.ds(h * 8 + s, 128, stride=16), :] for s in range(8)], axis=1
        )
        branch.append((outer[hrow, :] * filtered).astype(BF))
        hot_h = hot[a, :, h * 1024 : (h + 1) * 1024]
        hi, lo = split(gbranch[hrow, :] * filtered)
        gp2 += mm_nt(hot_h, hi) + mm_nt(hot_h, lo)
        ctt += mm_nt(hot_h, cot_ref[:, h * 1024 : (h + 1) * 1024])
    s_out[...] = (
        mm_tn(w_two[...], jnp.concatenate(branch, axis=0)).astype(BF).reshape(NT, 16, 1024)
    )
    x_out.start()
    r_out[b] = s_out[b]
    s_seg[0] = gp2
    s_seg[1] = ctt
    x_seg.start()
    r_seg[a] = s_seg[...]

    x_gg.recv()
    x_seg.recv()
    seg = jnp.sum(r_seg[...], axis=0)
    ctt = seg[1]
    hi, rest = seg[0].astype(BF), seg[0] - seg[0].astype(BF).astype(F32)
    mid, low_part = split(rest)
    row48, lane48 = iota2(48, 128)
    place = ones_at(((row48 & 15) + 32) == lane48).astype(BF)
    gp2_t = mm_tn(jnp.concatenate([hi, mid, low_part], axis=0), place)
    table = tall[...]
    swapped = jnp.where(lane128 < 16, pltpu.roll(table, 112, 1), pltpu.roll(table, 16, 1))
    grads = jnp.where(lane128 < 32, r_gg[...].reshape(128, 128) * swapped, gp2_t)
    gfirst = jnp.zeros((128, 128), F32)
    for p in range(3):
        hi, lo = split(jnp.where(p_lane == p, grads, 0.0))
        gfirst += mm(r_mix[p], hi) + mm(r_mix[p], lo)
    s_gt[...] = gfirst.reshape(NT, 8, 128)
    x_gt.start()
    r_gt[b] = s_gt[b]

    x_out.recv()
    mixture = mm_tn(w_back[...], r_out[...].reshape(256, 1024))
    for h in range(2):
        cols = slice(h * 1024, (h + 1) * 1024)
        embedded = mm_tn(emb_ref[...], hot[a, :, cols])
        lay_ref[:, cols] = (embedded + mixture[h * 128 : (h + 1) * 128]).astype(BF)

    x_gt.recv()
    gt = r_gt[...].reshape(128, 128).T
    gnt = jnp.zeros((16, 128), F32)
    for p in range(3):
        hi, lo = split(gt[p * 16 : (p + 1) * 16, :])
        block = blk_ref[:, p * 128 : (p + 1) * 128]
        gnt += mm_nt(hi, block) + mm_nt(lo, block)
    emb = emb_ref[...].astype(F32)
    scal_col = jnp.sum(jnp.where(lane16 == row16, scal_row, 0.0), axis=1, keepdims=True)
    ggrad_ref[...] = jnp.sum(gnt * emb * scal_col, axis=0, keepdims=True)
    s_cr[...] = jnp.broadcast_to(jnp.sum(gnt * gain_row * emb, axis=1, keepdims=True), (16, 128))
    x_cr.start()
    r_cr[b] = s_cr[...]

    x_fg.recv()
    grid_a[...] = r_fg[...].reshape(2048, 128).astype(F32)
    for q in range(16):
        fgrad_ref[:, q * 128 : (q + 1) * 128] = grid_a[pl.ds(q, 128, stride=16), :]

    x_cr.recv()
    cross = jnp.sum(r_cr[...], axis=0)
    egrad_ref[...] = (
        ctt
        + scal_col * gain_row * gnt
        - emb * (scal_col * scal_col * scal_col * cross * (1.0 / WIDTH))
    )

    for exchange in (
        x_filt, x_tok, x_gf, x_fl, x_fg, x_gg, x_seg, x_back, x_ss, x_tab, x_out, x_gt, x_cr
    ):
        exchange.drain()


def local(token_ids, embedding, norm_gain, proj_blocks, proj_mixers, out_blocks, out_mixers, filters, cotangent):
    vmem = pl.BlockSpec(memory_space=pltpu.VMEM)
    V = pltpu.VMEM
    scratch = [
        V((NC, 16, 2048), BF),
        V((NC, 16, 128), jnp.int32),
        V((NC, 16, 16, 128), BF), V((NC, 16, 16, 128), BF),
        V((NC, 16, 16, 128), BF), V((NC, 16, 16, 128), BF),
        V((NC, 16, 16, 128), BF), V((NC, 16, 16, 128), BF),
        V((16, 128), F32), V((NC, 16, 128), F32),
        V((2, 16, 128), F32), V((NC, 2, 16, 128), F32),
        V((NT, 16, 1024), BF), V((NT, 16, 1024), BF),
        V((8, 128), F32), V((NT, 8, 128), F32),
        V((NT, 8, 128), F32), V((NT, 8, 128), F32),
        V((NT, 16, 1024), BF), V((NT, 16, 1024), BF),
        V((NT, 8, 128), F32), V((NT, 8, 128), F32),
        V((16, 128), F32), V((NT, 16, 128), F32),
        V((256, 256), BF), V((256, 256), BF), V((3, 128, 128), BF),
        V((NC, 16, 2048), BF),
        V((128, 128), F32), V((128, 128), F32),
        V((2048, 128), F32), V((2048, 128), F32),
        V((16, 128, 256), F32), V((16, 128, 128), F32),
        V((256, 1024), F32), V((256, 1024), F32),
        pltpu.SemaphoreType.DMA((7, NC)), pltpu.SemaphoreType.DMA((7, NC)),
        pltpu.SemaphoreType.DMA((6, NT)), pltpu.SemaphoreType.DMA((6, NT)),
    ]
    layer_out, filter_grad, embed_grad, gain_grad = pl.pallas_call(
        kernel,
        out_shape=(
            jax.ShapeDtypeStruct((128, 2048), BF),
            jax.ShapeDtypeStruct((128, 2048), F32),
            jax.ShapeDtypeStruct((16, 128), F32),
            jax.ShapeDtypeStruct((1, 128), F32),
        ),
        in_specs=[vmem] * 15,
        out_specs=(vmem,) * 4,
        scratch_shapes=scratch,
        compiler_params=pltpu.CompilerParams(
            collective_id=0, has_side_effects=True, vmem_limit_bytes=56 * 1024 * 1024
        ),
    )(
        token_ids.reshape(16, 128),
        embedding,
        norm_gain.reshape(1, 128),
        proj_blocks.reshape(128, 384),
        proj_mixers.reshape(384, 16),
        out_blocks.reshape(128, 128),
        out_mixers.reshape(128, 16),
        filters,
        cotangent,
        *dft_tables(),
    )
    return layer_out, filter_grad, embed_grad, gain_grad.reshape(128)


def solution(mesh):
    in_specs = (
        P("ctx"),
        P(None, "tp"),
        P("tp"),
        P("tp", None, None),
        P(None, "tp", None, None),
        P("tp", None, None),
        P("tp", None, None),
        P("tp", "ctx"),
        P("tp", "ctx"),
    )
    out_specs = (P("tp", "ctx"), P("tp", "ctx"), P(None, "tp"), P("tp"))
    return jax.shard_map(local, mesh=mesh, in_specs=in_specs, out_specs=out_specs, check_vma=False)
```

time: 188 us -> 81.8 us (0.44)
  Pallas kernels: 0 us -> 76.8 us
  waiting for transfers between devices: 57.9 us -> 0 us
  starting transfers between devices: 56.2 us -> 0 us
  blocking collectives: 23.7 us -> 0 us
  matrix products: 17.9 us -> 0 us
  local copies, waits for them, and re-layouts: 21 us -> 4.14 us
  other arithmetic: 8.06 us -> 0 us
    pallas_call x0 -> x1, Pallas kernels: none -> 76.8 us  [local(): pl.pallas_call(kernel, out_shape=(jax.ShapeDtypeStruct((128, 2048), BF),...]
    all_to_all x11 -> x0, waiting for transfers between devices: 57.9 us -> none  [the longest x1 9.5 us: local(): lax.all_to_all(out_section.reshape(128, 1, tokens), 'tp', 0, 1, tiled=True)]
    all_to_all x11 -> x0, starting transfers between devices: 56.2 us -> none  [the longest x3 15.5 us: everyone(): lax.all_to_all(jnp.broadcast_to(x[None], (count,) + x.shape), axis, 0, 0,...]
    all_to_all x2 -> x0, blocking collectives: 23.7 us -> none  [everyone(): lax.all_to_all(jnp.broadcast_to(x[None], (count,) + x.shape), axis, 0, 0,...]
    dot_general x25 -> x0, matrix products: 16.4 us -> none  [the longest x15 9.51 us: dot(): jnp.einsum(formula, a.astype(BF), b.astype(BF), preferred_element_type=F32)]
    unnamed x80 -> x10, local copies, waits for them, and re-layouts: 12.4 us -> 4.14 us
    reshape x7 -> x0, local copies, waits for them, and re-layouts: 3.67 us -> none  [the longest x1 1.02 us: local(): filter_whole = filter_parts.transpose(1, 0, 2, 3).reshape(16, 128, 128)]
    another operation x5 -> x0, other arithmetic: 2.75 us -> none
  transfers between devices with their start and end apart: 11 -> 0, of which waited for: 10 -> 0; matrix products, arithmetic and copies ran while one was open for 14% -> 0% of each run, Pallas kernels for 0% -> 0%
where the time goes in v1:
time: 81.8 us; the launch traced here: 81.6 us
  Pallas kernels  76.8 us (94%)
  local copies, waits for them, and re-layouts  4.14 us (5%)
    pallas_call x1, Pallas kernels, local(): pl.pallas_call(kernel, out_shape=(jax.ShapeDtypeStruct((128, 2048), BF),...  76.8 us
    unnamed x10, local copies, waits for them, and re-layouts  4.14 us

profile of v1, /device:TPU:1, one launch (start us, length us, event | category | flops | bytes accessed | tf_op | source)
XLA Modules:
  0.0 81.6 jit_solution(16917709487845830045)
XLA Ops:
  0.6 76.8 %shard_map.174 = (bf16[128,2048]{1,0:T(8,128)(2,1)}, f32[128,2048]{1,0:T(8,128)}, f32[16,128]{1,0:T(8,128)}, f32[1,128]{1,0:T(1,128)}) custom-call(s32[16,128]{1,0:T(8,128)} %bitcast.11, bf16[16,128]{1,0:T(8,128)(2,1)} %emb_ref.1, f32[1,128]{1,0:T(1,128)} %bitcast.12, bf16[128,384]{1,0:T(8,128)(2,1)} %bitcast.7, bf16[384,16]{1,0:T(8,128)(2,1)} %bitcast.8, ...), custom_call_target="tpu_custom_call" | custom-call | tf_op jit(solution)/shard_map/pallas_call | solution.py:430
  77.4 0.0 copy-start
  77.5 2.0 %copy.23 = bf16[128,2048]{1,0:T(8,128)(2,1)} copy(bf16[128,2048]{1,0:T(8,128)(2,1)} %get-tuple-element.16) | data formatting | bytes 1048576
  79.4 0.0 copy-done
  79.4 0.0 copy-start.1
  79.4 1.0 %copy.24 = f32[128,2048]{1,0:T(8,128)} copy(f32[128,2048]{1,0:T(8,128)S(1)} %copy-done) | data formatting | bytes 2097152
  80.4 0.0 copy-done.1
  80.4 0.0 copy-start.2
  80.4 0.6 copy.25
  81.0 0.1 copy-done.2
  81.1 0.5 copy.26
Async XLA Ops:
  77.4 2.0 %copy-start = (f32[128,2048]{1,0:T(8,128)S(1)}, f32[128,2048]{1,0:T(8,128)}, u32[]{:S(2)}) copy-start(f32[128,2048]{1,0:T(8,128)} %get-tuple-element.17) | copy-start | bytes 3145732
  79.4 1.0 %copy-start.1 = (f32[16,128]{1,0:T(8,128)S(1)}, f32[16,128]{1,0:T(8,128)}, u32[]{:S(2)}) copy-start(f32[16,128]{1,0:T(8,128)} %get-tuple-element.18) | copy-start | bytes 24580
  80.4 0.7 copy-start.2

commit v2 on v1

--- a/solution.py
+++ b/solution.py
@@ -15,8 +15,8 @@
 F32 = jnp.float32
 MESH = pl.DeviceIdType.MESH
 
-FILT_IN, TOK, GF, FILT, FG, GG, SEG = range(7)
-BACK, SS, TAB, OUT, GT, CR = range(6)
+FILT_IN, TOK, GF, GG, SEG, FILT, FG = 0, 1, 2, 3, 4, 5, 9
+BACK, SS, TAB, OUT, GT = range(5)
 
 
 def dft_tables():
@@ -33,11 +33,8 @@
     cast = lambda a, d: jnp.asarray(a, F32).astype(d)
     return (
         cast(c1, BF),
-        cast(np.cos(twist), F32),
-        cast(np.sin(twist), F32),
-        cast(c2, BF),
-        cast(i1, BF),
-        cast(i2, BF),
+        cast(np.concatenate([np.cos(twist), np.sin(twist)], 1), F32),
+        cast(np.concatenate([c2, i1, i2], 0), BF),
     )
 
 
@@ -70,13 +67,14 @@
 
 
 def kernel(
-    tok_ref, emb_ref, gain_ref, blk_ref, mix_ref, oblk_ref, omix_ref, filt_ref, cot_ref,
-    c1_ref, tc_ref, ts_ref, c2_ref, i1_ref, i2_ref,
-    lay_ref, fgrad_ref, egrad_ref, ggrad_ref,
-    r_filt, r_tok, s_gf, r_gf, s_fl, r_fl, s_fg, r_fg, s_gg, r_gg, s_seg, r_seg,
-    s_back, r_back, s_ss, r_ss, s_tab, r_tab, s_out, r_out, s_gt, r_gt, s_cr, r_cr,
-    w_back, w_two, r_mix, hot, tall, gated_t, grid_a, grid_b, spec_x, spec_s, outer, gbranch,
-    ssem_c, rsem_c, ssem_t, rsem_t,
+    tok_hbm, emb_hbm, gain_hbm, blk_hbm, mix_hbm, oblk_hbm, omix_hbm, filt_hbm, cot_hbm,
+    c1_hbm, turn_hbm, dft_hbm,
+    r_out, r_fg, w_back, embedded, small,
+    tok_ref, emb_ref, gain_ref, blk_ref, mix_ref, oblk_ref, omix_ref, cot_ref, c1_ref, turn_ref, dft_ref,
+    r_filt, r_tok, s_gf, r_gf, s_fl, r_fl, s_fg, s_gg, r_gg, s_seg, r_seg,
+    s_back, r_back, s_ss, r_ss, s_tab, r_tab, s_out, s_gt, r_gt,
+    w_two, r_mix, hot, tall, gated_t, grid_a, grid_b, spec_x, spec_g, spec_s, outer, gbranch,
+    ssem_c, rsem_c, ssem_t, rsem_t, lsem,
 ):
     a = lax.axis_index("ctx")
     b = lax.axis_index("tp")
@@ -119,11 +117,12 @@
     slot = lambda ref: (lambda p: ref.at[p])
     whole = lambda ref: (lambda p: ref)
 
-    x_filt = Exchange("ctx", FILT_IN, rows16(filt_ref), slot(r_filt))
+    x_filt = Exchange("ctx", FILT_IN, rows16(filt_hbm), slot(r_filt))
     x_tok = Exchange("ctx", TOK, whole(tok_ref), slot(r_tok))
     x_gf = Exchange("ctx", GF, slot(s_gf), slot(r_gf))
-    x_fl = Exchange("ctx", FILT, slot(s_fl), slot(r_fl))
-    x_fg = Exchange("ctx", FG, slot(s_fg), slot(r_fg))
+    quarter = lambda ref, n: (lambda p: ref.at[p, pl.ds(n * 4, 4)])
+    x_fl = lambda n: Exchange("ctx", FILT + n, quarter(s_fl, n), quarter(r_fl, n))
+    x_fg = lambda n: Exchange("ctx", FG + n, quarter(s_fg, n), quarter(r_fg, n))
     x_gg = Exchange("ctx", GG, whole(s_gg), slot(r_gg))
     x_seg = Exchange("ctx", SEG, whole(s_seg), slot(r_seg))
     x_back = Exchange("tp", BACK, slot(s_back), slot(r_back))
@@ -131,7 +130,6 @@
     x_tab = Exchange("tp", TAB, slot(s_tab), slot(r_tab))
     x_out = Exchange("tp", OUT, slot(s_out), slot(r_out))
     x_gt = Exchange("tp", GT, slot(s_gt), slot(r_gt))
-    x_cr = Exchange("tp", CR, whole(s_cr), slot(r_cr))
 
     barrier = pltpu.get_barrier_semaphore()
 
@@ -147,21 +145,38 @@
     greet("ctx", a, NC)
     greet("tp", b, NT)
 
+    own = pl.ds(pl.multiple_of(a * 16, 16), 16)
+    loads = {}
+    for n, (name, src, dst) in enumerate(
+        (
+            ("omix", omix_hbm, omix_ref),
+            ("cot", cot_hbm, cot_ref),
+            ("emb", emb_hbm, emb_ref),
+            ("tok", tok_hbm, tok_ref),
+            ("filt", filt_hbm.at[own, :], r_filt.at[a]),
+            ("mix", mix_hbm, mix_ref),
+            ("gain", gain_hbm, gain_ref),
+            ("blk", blk_hbm, blk_ref),
+            ("oblk", oblk_hbm, oblk_ref),
+            ("c1", c1_hbm, c1_ref),
+            ("turn", turn_hbm, turn_ref),
+            ("dft", dft_hbm, dft_ref),
+        )
+    ):
+        loads[name] = pltpu.make_async_copy(src, dst, lsem.at[n])
+        loads[name].start()
+
     row128, lane128 = iota2(128, 128)
     p_lane = lane128 >> 4
 
     row16, lane16 = iota2(16, 128)
     spread = ones_at(((lane16 & 15) == row16) & (lane16 < 48)).astype(BF)
+    loads["emb"].wait()
+    loads["tok"].wait()
     emb_t = mm_tn(emb_ref[...], spread)
     s_ss[...] = jnp.broadcast_to(jnp.sum(emb_t * emb_t, axis=0, keepdims=True), (8, 128))
 
-    pl.semaphore_wait(barrier, NC - 1 + NT - 1)
-    x_ss.start()
-    x_tok.start()
-    x_filt.start()
-    r_ss[b] = s_ss[...]
-    r_tok[a] = tok_ref[...]
-
+    loads["omix"].wait()
     tile_m = ones_at((lane16 & 15) == row16).astype(BF)
     row, lane = iota2(256, 128)
     sel_row = ones_at(((row & 7) == (lane >> 4)) & ((row >> 4) == (lane & 15))).astype(BF)
@@ -169,16 +184,26 @@
     row, lane = iota2(256, 256)
     keep = ((row & 7) == ((lane >> 4) & 7)) & (((row >> 3) & 1) == (lane >> 7))
     w_back[...] = jnp.where(keep, jnp.concatenate([wide, wide], axis=1), 0.0).astype(BF)
+    loads["cot"].wait()
     cot2 = jnp.concatenate([cot_ref[:, :1024], cot_ref[:, 1024:]], axis=0)
     s_back[...] = mm(w_back[...], cot2).astype(BF).reshape(NT, 16, 1024)
+    pl.semaphore_wait(barrier, NC - 1 + NT - 1)
+    x_ss.start()
+    x_tok.start()
     x_back.start()
+    x_filt.start()
+    r_ss[b] = s_ss[...]
+    r_tok[a] = tok_ref[...]
+
     r_back[b] = s_back[b]
-    r_filt[a] = filt_ref[pl.ds(pl.multiple_of(a * 16, 16), 16), :]
 
     sel_p = ones_at(((row128 & 7) == p_lane) & ((row128 >> 3) == (lane128 & 15))).astype(BF)
+    loads["mix"].wait()
     for p in range(3):
         wide = mm(sel_p, mm(mix_ref[p * 128 : (p + 1) * 128, :], tile_m).astype(BF))
         r_mix[p] = jnp.where((row128 & 7) == p_lane, wide, 0.0).astype(BF)
+    for name in ("gain", "blk", "oblk", "c1", "turn", "dft", "filt"):
+        loads[name].wait()
     gain_row = gain_ref[...]
     gain_col = jnp.sum(jnp.where(row128 == lane128, gain_row, 0.0), axis=1, keepdims=True)
 
@@ -191,7 +216,7 @@
         first += mm_tn(
             blk_ref[:, p * 128 : (p + 1) * 128], jnp.where(p_lane == p, normed, 0.0).astype(BF)
         )
-    s_tab[...] = first.astype(BF).astype(F32).reshape(NT, 8, 128)
+    s_tab[...] = first.reshape(NT, 8, 128)
     x_tab.start()
     r_tab[b] = s_tab[b]
 
@@ -223,6 +248,7 @@
     for h in range(2):
         hot_h = hot[a, :, h * 1024 : (h + 1) * 1024]
         outer[h * 128 : (h + 1) * 128, :] = mm(outer_w, jnp.concatenate([hot_h, hot_h], axis=0))
+        embedded[h * 128 : (h + 1) * 128, :] = mm_tn(emb_ref[...], hot_h).astype(BF)
 
     x_back.recv()
     gbranch[...] = mm(w_two[...], r_back[...].reshape(256, 1024))
@@ -241,36 +267,61 @@
         for q in range(16):
             grid_a[pl.ds(src * 16 + q, 16, stride=128), :] = vals[:, q * 128 : (q + 1) * 128]
 
-    tc = tc_ref[...]
-    ts = ts_ref[...]
-
-    def forward(signal, second):
-        first_stage = mm(c1_ref[...], signal)
-        re, im = first_stage[:128], first_stage[128:]
-        turned = jnp.concatenate([re * tc + im * ts, im * tc - re * ts], axis=1)
-        return mm(turned.astype(BF), second)
+    tc = turn_ref[:, :128]
+    ts = turn_ref[:, 128:]
+    c2_ref = dft_ref.at[0:256, :]
+    i1_ref = dft_ref.at[256:512, :]
+    i2_ref = dft_ref.at[512:640, :]
+    tc2 = jnp.concatenate([tc, tc], axis=1)
+    ts2 = jnp.concatenate([ts, ts], axis=1)
+
+    def forward(signals, second):
+        turned = []
+        for u in range(0, len(signals), 2):
+            stage = mm(c1_ref[...], jnp.concatenate(signals[u : u + 2], axis=1))
+            re, im = stage[:128], stage[128:]
+            tr = re * tc2 + im * ts2
+            ti = im * tc2 - re * ts2
+            for v in range(2):
+                cols = slice(v * 128, (v + 1) * 128)
+                turned.append(jnp.concatenate([tr[:, cols], ti[:, cols]], axis=1).astype(BF))
+        return mm(jnp.concatenate(turned, axis=0), second)
 
     def inverse(spectrum, weights):
         back = mm(spectrum.astype(BF), weights)
-        re, im = back[:, :128], back[:, 128:]
-        turned = jnp.concatenate([re * tc - im * ts, im * tc + re * ts], axis=0)
-        return mm(i2_ref[...], turned.astype(BF))
-
-    def channels(step, body):
-        def block(n, carry):
-            for u in range(step):
-                body(n * step + u)
+        results = []
+        for u in range(0, spectrum.shape[0], 256):
+            both = [
+                jnp.concatenate(
+                    [back[u + v : u + v + 128, :128], back[u + v : u + v + 128, 128:]], axis=0
+                )
+                for v in (0, 128)
+            ]
+            both = jnp.concatenate(both, axis=1)
+            re, im = both[:128], both[128:]
+            turned = jnp.concatenate([re * tc2 - im * ts2, im * tc2 + re * ts2], axis=0)
+            pair = mm(i2_ref[...], turned.astype(BF))
+            results += [pair[:, :128], pair[:, 128:]]
+        return results
+
+    def groups(body):
+        def step(n, carry):
+            body(n)
             return carry
 
-        lax.fori_loop(0, 16 // step, block, 0)
-
-    def at_rows(ref, c):
-        return ref.at[pl.ds(pl.multiple_of(c * 128, 128), 128), :]
-
-    def gated_spectrum(c):
-        spec_x[c] = forward(at_rows(grid_a, c)[...].astype(BF), c2_ref[...])
-
-    channels(4, gated_spectrum)
+        lax.fori_loop(0, 4, step, 0)
+
+    def rows_of(n):
+        return pl.ds(pl.multiple_of(n * 512, 512), 512)
+
+    def signals(ref, n):
+        block = ref[rows_of(n), :].astype(BF)
+        return [block[u * 128 : (u + 1) * 128] for u in range(4)]
+
+    def gated_spectrum(n):
+        spec_x[rows_of(n), :] = forward(signals(grid_a, n), c2_ref[...])
+
+    groups(gated_spectrum)
 
     x_filt.recv()
     for src in range(NC):
@@ -279,44 +330,33 @@
                 src, :, q * 128 : (q + 1) * 128
             ].astype(F32)
 
-    def filtered_channel(c):
-        even = 2.0 * forward(at_rows(grid_b, c)[...].astype(BF), c2_ref[:, :128])
-        spec_s[c] = even
-        spectrum = spec_x[c] * jnp.concatenate([even, even], axis=1)
-        s_fl[:, c] = inverse(spectrum, i1_ref[...]).astype(BF).reshape(NC, 16, 128)
-
-    channels(4, filtered_channel)
-    x_fl.start()
+    def filtered_group(n):
+        even = 2.0 * forward(signals(grid_b, n), c2_ref[:, :128])
+        spec_s[rows_of(n), :] = even
+        spectrum = spec_x[rows_of(n), :] * jnp.concatenate([even, even], axis=1)
+        for u, result in enumerate(inverse(spectrum, i1_ref[...])):
+            s_fl[:, n * 4 + u] = result.astype(BF).reshape(NC, 16, 128)
+        x_fl(n).start()
+
+    groups(filtered_group)
     r_fl[a] = s_fl[a]
 
     x_gf.recv()
 
-    def grad_channel(c):
-        spec_g = forward(r_gf[:, c].reshape(128, 128), c2_ref[...])
-        even = spec_s[c]
-        prod = spec_g * spec_x[c]
+    def grad_group(n):
+        spectrum = forward([r_gf[:, n * 4 + u].reshape(128, 128) for u in range(4)], c2_ref[...])
+        spec_g[rows_of(n), :] = spectrum
+        prod = spectrum * spec_x[rows_of(n), :]
         cross = 2.0 * (prod[:, :128] + prod[:, 128:])
-        s_fg[:, c] = inverse(cross, i1_ref[:128, :]).astype(BF).reshape(NC, 16, 128)
-        at_rows(grid_b, c)[...] = inverse(
-            spec_g * jnp.concatenate([even, even], axis=1), i1_ref[...]
-        )
-
-    channels(2, grad_channel)
-    x_fg.start()
+        for u, result in enumerate(inverse(cross, i1_ref[:128, :])):
+            s_fg[:, n * 4 + u] = result.astype(BF).reshape(NC, 16, 128)
+        x_fg(n).start()
+
+    groups(grad_group)
     r_fg[a] = s_fg[a]
 
-    sums = jnp.zeros((16, 32), F32)
-    for src in range(NC):
-        vals = jnp.concatenate(
-            [grid_b[pl.ds(src * 16 + q, 16, stride=128), :] for q in range(16)], axis=1
-        ).astype(BF)
-        hot_s = hot[src]
-        sums += mm_nt(vals, jnp.concatenate([hot_s, hot_s], axis=0))
-    s_gg[...] = jnp.concatenate([sums, jnp.zeros((16, 96), F32)], axis=1)
-    x_gg.start()
-    r_gg[a] = s_gg[...]
-
-    x_fl.recv()
+    for n in range(4):
+        x_fl(n).recv()
     grid_a[...] = r_fl[...].reshape(2048, 128).astype(F32)
     gp2 = jnp.zeros((16, 128), F32)
     ctt = jnp.zeros((16, 128), F32)
@@ -331,15 +371,34 @@
         hi, lo = split(gbranch[hrow, :] * filtered)
         gp2 += mm_nt(hot_h, hi) + mm_nt(hot_h, lo)
         ctt += mm_nt(hot_h, cot_ref[:, h * 1024 : (h + 1) * 1024])
-    s_out[...] = (
-        mm_tn(w_two[...], jnp.concatenate(branch, axis=0)).astype(BF).reshape(NT, 16, 1024)
-    )
-    x_out.start()
-    r_out[b] = s_out[b]
     s_seg[0] = gp2
     s_seg[1] = ctt
     x_seg.start()
     r_seg[a] = s_seg[...]
+    s_out[...] = (
+        mm_tn(w_two[...], jnp.concatenate(branch, axis=0)).astype(BF).reshape(NT, 16, 1024)
+    )
+    x_out.start()
+    r_out[b] = s_out[b]
+
+    def gated_group(n):
+        even = spec_s[rows_of(n), :]
+        spectrum = spec_g[rows_of(n), :] * jnp.concatenate([even, even], axis=1)
+        for u, result in enumerate(inverse(spectrum, i1_ref[...])):
+            start = pl.multiple_of(n * 512 + u * 128, 128)
+            grid_b[pl.ds(start, 128), :] = result
+
+    groups(gated_group)
+    sums = jnp.zeros((16, 32), F32)
+    for src in range(NC):
+        vals = jnp.concatenate(
+            [grid_b[pl.ds(src * 16 + q, 16, stride=128), :] for q in range(16)], axis=1
+        ).astype(BF)
+        hot_s = hot[src]
+        sums += mm_nt(vals, jnp.concatenate([hot_s, hot_s], axis=0))
+    s_gg[...] = jnp.concatenate([sums, jnp.zeros((16, 96), F32)], axis=1)
+    x_gg.start()
+    r_gg[a] = s_gg[...]
 
     x_gg.recv()
     x_seg.recv()
@@ -357,16 +416,14 @@
     for p in range(3):
         hi, lo = split(jnp.where(p_lane == p, grads, 0.0))
         gfirst += mm(r_mix[p], hi) + mm(r_mix[p], lo)
-    s_gt[...] = gfirst.reshape(NT, 8, 128)
+    share = jnp.sum(gfirst * r_tab[...].reshape(128, 128), axis=0, keepdims=True) / scal_row
+    share = jnp.broadcast_to(share, (128, 128))
+    share = pltpu.roll(share, 48, 1) + pltpu.roll(share, 32, 1) + pltpu.roll(share, 16, 1)
+    s_gt[...] = jnp.where(
+        lane128 < 48, gfirst, jnp.where(lane128 < 64, share, 0.0)
+    ).reshape(NT, 8, 128)
     x_gt.start()
     r_gt[b] = s_gt[b]
-
-    x_out.recv()
-    mixture = mm_tn(w_back[...], r_out[...].reshape(256, 1024))
-    for h in range(2):
-        cols = slice(h * 1024, (h + 1) * 1024)
-        embedded = mm_tn(emb_ref[...], hot[a, :, cols])
-        lay_ref[:, cols] = (embedded + mixture[h * 128 : (h + 1) * 128]).astype(BF)
 
     x_gt.recv()
     gt = r_gt[...].reshape(128, 128).T
@@ -375,68 +432,94 @@
         hi, lo = split(gt[p * 16 : (p + 1) * 16, :])
         block = blk_ref[:, p * 128 : (p + 1) * 128]
         gnt += mm_nt(hi, block) + mm_nt(lo, block)
+    cross = jnp.sum(gt[48:64, :], axis=1, keepdims=True) * 0.125
     emb = emb_ref[...].astype(F32)
     scal_col = jnp.sum(jnp.where(lane16 == row16, scal_row, 0.0), axis=1, keepdims=True)
-    ggrad_ref[...] = jnp.sum(gnt * emb * scal_col, axis=0, keepdims=True)
-    s_cr[...] = jnp.broadcast_to(jnp.sum(gnt * gain_row * emb, axis=1, keepdims=True), (16, 128))
-    x_cr.start()
-    r_cr[b] = s_cr[...]
-
-    x_fg.recv()
-    grid_a[...] = r_fg[...].reshape(2048, 128).astype(F32)
-    for q in range(16):
-        fgrad_ref[:, q * 128 : (q + 1) * 128] = grid_a[pl.ds(q, 128, stride=16), :]
-
-    x_cr.recv()
-    cross = jnp.sum(r_cr[...], axis=0)
-    egrad_ref[...] = (
+    small[16:24, :] = jnp.broadcast_to(
+        jnp.sum(gnt * emb * scal_col, axis=0, keepdims=True), (8, 128)
+    )
+    small[0:16, :] = (
         ctt
         + scal_col * gain_row * gnt
         - emb * (scal_col * scal_col * scal_col * cross * (1.0 / WIDTH))
     )
 
+    x_out.recv()
+    for n in range(4):
+        x_fg(n).recv()
+
     for exchange in (
-        x_filt, x_tok, x_gf, x_fl, x_fg, x_gg, x_seg, x_back, x_ss, x_tab, x_out, x_gt, x_cr
+        x_filt, x_tok, x_gf, x_gg, x_seg, x_back, x_ss, x_tab, x_out, x_gt,
+        *[x_fl(n) for n in range(4)], *[x_fg(n) for n in range(4)],
     ):
         exchange.drain()
+
+
+def finish(
+    out_hbm, fg_hbm, w_hbm, emb_hbm, small_hbm,
+    lay_ref, fgrad_ref, egrad_ref, ggrad_ref,
+    out_ref, fg_ref, w_ref, emb_ref, small_ref, grid, sem,
+):
+    pairs = (
+        (fg_hbm, fg_ref), (out_hbm, out_ref), (w_hbm, w_ref), (emb_hbm, emb_ref),
+        (small_hbm, small_ref),
+    )
+    copies = [pltpu.make_async_copy(src, dst, sem.at[n]) for n, (src, dst) in enumerate(pairs)]
+    for copy in copies:
+        copy.start()
+    copies[0].wait()
+    grid[...] = fg_ref[...].reshape(2048, 128).astype(F32)
+    for q in range(16):
+        fgrad_ref[:, q * 128 : (q + 1) * 128] = grid[pl.ds(q, 128, stride=16), :]
+    for copy in copies[1:]:
+        copy.wait()
+    mixture = mm_tn(w_ref[...], out_ref[...].reshape(256, 1024))
+    for h in range(2):
+        hrow = slice(h * 128, (h + 1) * 128)
+        lay_ref[:, h * 1024 : (h + 1) * 1024] = (emb_ref[hrow].astype(F32) + mixture[hrow]).astype(BF)
+    egrad_ref[...] = small_ref[0:16, :]
+    ggrad_ref[...] = small_ref[16:17, :]
 
 
 def local(token_ids, embedding, norm_gain, proj_blocks, proj_mixers, out_blocks, out_mixers, filters, cotangent):
     vmem = pl.BlockSpec(memory_space=pltpu.VMEM)
     V = pltpu.VMEM
     scratch = [
+        V((16, 128), jnp.int32), V((16, 128), BF), V((1, 128), F32), V((128, 384), BF),
+        V((384, 16), BF), V((128, 128), BF), V((128, 16), BF), V((128, 2048), BF),
+        V((256, 128), BF), V((128, 256), F32), V((640, 256), BF),
         V((NC, 16, 2048), BF),
         V((NC, 16, 128), jnp.int32),
         V((NC, 16, 16, 128), BF), V((NC, 16, 16, 128), BF),
         V((NC, 16, 16, 128), BF), V((NC, 16, 16, 128), BF),
-        V((NC, 16, 16, 128), BF), V((NC, 16, 16, 128), BF),
+        V((NC, 16, 16, 128), BF),
         V((16, 128), F32), V((NC, 16, 128), F32),
         V((2, 16, 128), F32), V((NC, 2, 16, 128), F32),
         V((NT, 16, 1024), BF), V((NT, 16, 1024), BF),
         V((8, 128), F32), V((NT, 8, 128), F32),
         V((NT, 8, 128), F32), V((NT, 8, 128), F32),
-        V((NT, 16, 1024), BF), V((NT, 16, 1024), BF),
+        V((NT, 16, 1024), BF),
         V((NT, 8, 128), F32), V((NT, 8, 128), F32),
-        V((16, 128), F32), V((NT, 16, 128), F32),
-        V((256, 256), BF), V((256, 256), BF), V((3, 128, 128), BF),
+        V((256, 256), BF), V((3, 128, 128), BF),
         V((NC, 16, 2048), BF),
         V((128, 128), F32), V((128, 128), F32),
         V((2048, 128), F32), V((2048, 128), F32),
-        V((16, 128, 256), F32), V((16, 128, 128), F32),
+        V((2048, 256), F32), V((2048, 256), F32), V((2048, 128), F32),
         V((256, 1024), F32), V((256, 1024), F32),
-        pltpu.SemaphoreType.DMA((7, NC)), pltpu.SemaphoreType.DMA((7, NC)),
-        pltpu.SemaphoreType.DMA((6, NT)), pltpu.SemaphoreType.DMA((6, NT)),
+        pltpu.SemaphoreType.DMA((13, NC)), pltpu.SemaphoreType.DMA((13, NC)),
+        pltpu.SemaphoreType.DMA((5, NT)), pltpu.SemaphoreType.DMA((5, NT)), pltpu.SemaphoreType.DMA((12,)),
     ]
-    layer_out, filter_grad, embed_grad, gain_grad = pl.pallas_call(
+    received = pl.pallas_call(
         kernel,
         out_shape=(
-            jax.ShapeDtypeStruct((128, 2048), BF),
-            jax.ShapeDtypeStruct((128, 2048), F32),
-            jax.ShapeDtypeStruct((16, 128), F32),
-            jax.ShapeDtypeStruct((1, 128), F32),
+            jax.ShapeDtypeStruct((NT, 16, 1024), BF),
+            jax.ShapeDtypeStruct((NC, 16, 16, 128), BF),
+            jax.ShapeDtypeStruct((256, 256), BF),
+            jax.ShapeDtypeStruct((256, 1024), BF),
+            jax.ShapeDtypeStruct((24, 128), F32),
         ),
-        in_specs=[vmem] * 15,
-        out_specs=(vmem,) * 4,
+        in_specs=[pl.BlockSpec(memory_space=pltpu.HBM)] * 12,
+        out_specs=(vmem,) * 5,
         scratch_shapes=scratch,
         compiler_params=pltpu.CompilerParams(
             collective_id=0, has_side_effects=True, vmem_limit_bytes=56 * 1024 * 1024
@@ -453,6 +536,22 @@
         cotangent,
         *dft_tables(),
     )
+    layer_out, filter_grad, embed_grad, gain_grad = pl.pallas_call(
+        finish,
+        out_shape=(
+            jax.ShapeDtypeStruct((128, 2048), BF),
+            jax.ShapeDtypeStruct((128, 2048), F32),
+            jax.ShapeDtypeStruct((16, 128), F32),
+            jax.ShapeDtypeStruct((1, 128), F32),
+        ),
+        in_specs=[pl.BlockSpec(memory_space=pltpu.HBM)] * 5,
+        out_specs=(vmem,) * 4,
+        scratch_shapes=[
+            V((NT, 16, 1024), BF), V((NC, 16, 16, 128), BF), V((256, 256), BF), V((256, 1024), BF),
+            V((24, 128), F32), V((2048, 128), F32), pltpu.SemaphoreType.DMA((5,)),
+        ],
+        compiler_params=pltpu.CompilerParams(vmem_limit_bytes=56 * 1024 * 1024),
+    )(*received)
     return layer_out, filter_grad, embed_grad, gain_grad.reshape(128)
 
 

time: 81.8 us -> 70.7 us (0.86)
  Pallas kernels: 76.8 us -> 69.9 us
  local copies, waits for them, and re-layouts: 4.14 us -> 0 us
    pallas_call x1 -> x2, Pallas kernels: 76.8 us -> 69.9 us  [the longest x1 67.3 us: local(): pl.pallas_call(kernel, out_shape=(jax.ShapeDtypeStruct((NT, 16, 1024), BF...]
    unnamed x10 -> x0, local copies, waits for them, and re-layouts: 4.14 us -> none
where the time goes in v2:
time: 70.7 us; the launch traced here: 70.6 us
  Pallas kernels  69.9 us (99%)
    pallas_call x1, Pallas kernels, local(): pl.pallas_call(kernel, out_shape=(jax.ShapeDtypeStruct((NT, 16, 1024), BF...  67.3 us
    pallas_call x1, Pallas kernels, local(): pl.pallas_call(finish, out_shape=(jax.ShapeDtypeStruct((128, 2048), BF),...  2.64 us

profile of v2, /device:TPU:1, one launch (start us, length us, event | category | flops | bytes accessed | tf_op | source)
XLA Modules:
  0.0 70.6 jit_solution(15979409228376093709)
XLA Ops:
  0.6 67.3 %shard_map.147 = (bf16[16,16,1024]{2,1,0:T(8,128)(2,1)}, bf16[8,16,16,128]{3,2,1,0:T(8,128)(2,1)}, bf16[256,256]{1,0:T(8,128)(2,1)}, bf16[256,1024]{1,0:T(8,128)(2,1)}, f32[24,128]{1,0:T(8,128)}) custom-call(s32[16,128]{1,0:T(8,128)} %bitcast.11, bf16[16,128]{1,0:T(8,128)(2,1)} %emb_hbm.1, f32[1,128]{1,0:T(1,128)} %bitcast.12, bf16[128,384]{1,0:T(8,128)(2,1)} %bitcast.7, ...), custom_call_target="tpu_custom_call" | custom-call | tf_op jit(solution)/shard_map/pallas_call | solution.py:512
  67.9 2.6 %shard_map.148 = (bf16[128,2048]{1,0:T(8,128)(2,1)}, f32[128,2048]{1,0:T(8,128)}, f32[16,128]{1,0:T(8,128)}, f32[1,128]{1,0:T(1,128)}) custom-call(bf16[16,16,1024]{2,1,0:T(8,128)(2,1)} %get-tuple-element.13.out_hbm, bf16[8,16,16,128]{3,2,1,0:T(8,128)(2,1)} %get-tuple-element.14.fg_hbm, bf16[256,256]{1,0:T(8,128)(2,1)} %get-tuple-element.15.w_hbm, ...), custom_call_target="tpu_custom_call" | custom-call | tf_op jit(solution)/shard_map/pallas_call | solution.py:539

commit v3 on v2

--- a/solution.py
+++ b/solution.py
@@ -16,7 +16,7 @@
 MESH = pl.DeviceIdType.MESH
 
 FILT_IN, TOK, GF, GG, SEG, FILT, FG = 0, 1, 2, 3, 4, 5, 9
-BACK, SS, TAB, OUT, GT = range(5)
+BACK, TAB, OUT, GT = range(4)
 
 
 def dft_tables():
@@ -72,20 +72,25 @@
     r_out, r_fg, w_back, embedded, small,
     tok_ref, emb_ref, gain_ref, blk_ref, mix_ref, oblk_ref, omix_ref, cot_ref, c1_ref, turn_ref, dft_ref,
     r_filt, r_tok, s_gf, r_gf, s_fl, r_fl, s_fg, s_gg, r_gg, s_seg, r_seg,
-    s_back, r_back, s_ss, r_ss, s_tab, r_tab, s_out, s_gt, r_gt,
+    s_back, r_back, s_tab, r_tab, s_out, s_gt, r_gt,
     w_two, r_mix, hot, tall, gated_t, grid_a, grid_b, spec_x, spec_g, spec_s, outer, gbranch,
     ssem_c, rsem_c, ssem_t, rsem_t, lsem,
 ):
     a = lax.axis_index("ctx")
     b = lax.axis_index("tp")
 
+    def peer_of(axis, k):
+        if axis == "tp":
+            return lax.rem(b + k, NT)
+        return lax.rem(a // 4 + k // 4, 2) * 4 + lax.rem(a % 4 + k % 4, 4)
+
     class Exchange:
         def __init__(self, axis, msg, src, dst):
             self.me, self.n = (a, NC) if axis == "ctx" else (b, NT)
             sends, recvs = (ssem_c, rsem_c) if axis == "ctx" else (ssem_t, rsem_t)
 
             def copy(k):
-                peer = lax.rem(self.me + k, self.n)
+                peer = peer_of(axis, k)
                 return pltpu.make_async_remote_copy(
                     src_ref=src(peer),
                     dst_ref=dst(self.me),
@@ -97,15 +102,15 @@
 
             self.copy = copy
 
-        def each(self, act):
+        def each(self, act, low=1, high=None):
             def body(k, carry):
                 act(self.copy(k))
                 return carry
 
-            lax.fori_loop(1, self.n, body, 0)
-
-        def start(self):
-            self.each(lambda c: c.start())
+            lax.fori_loop(low, high or self.n, body, 0)
+
+        def start(self, low=1, high=None):
+            self.each(lambda c: c.start(), low, high)
 
         def recv(self):
             self.each(lambda c: c.wait_recv())
@@ -126,41 +131,40 @@
     x_gg = Exchange("ctx", GG, whole(s_gg), slot(r_gg))
     x_seg = Exchange("ctx", SEG, whole(s_seg), slot(r_seg))
     x_back = Exchange("tp", BACK, slot(s_back), slot(r_back))
-    x_ss = Exchange("tp", SS, whole(s_ss), slot(r_ss))
     x_tab = Exchange("tp", TAB, slot(s_tab), slot(r_tab))
     x_out = Exchange("tp", OUT, slot(s_out), slot(r_out))
     x_gt = Exchange("tp", GT, slot(s_gt), slot(r_gt))
 
     barrier = pltpu.get_barrier_semaphore()
 
-    def greet(axis, me, n):
+    def greet(axis, n):
         def body(k, carry):
             pl.semaphore_signal(
-                barrier, inc=1, device_id={axis: lax.rem(me + k, n)}, device_id_type=MESH
+                barrier, inc=1, device_id={axis: peer_of(axis, k)}, device_id_type=MESH
             )
             return carry
 
         lax.fori_loop(1, n, body, 0)
 
-    greet("ctx", a, NC)
-    greet("tp", b, NT)
+    greet("ctx", NC)
+    greet("tp", NT)
 
     own = pl.ds(pl.multiple_of(a * 16, 16), 16)
     loads = {}
     for n, (name, src, dst) in enumerate(
         (
+            ("emb", emb_hbm, emb_ref),
+            ("gain", gain_hbm, gain_ref),
+            ("blk", blk_hbm, blk_ref),
             ("omix", omix_hbm, omix_ref),
             ("cot", cot_hbm, cot_ref),
-            ("emb", emb_hbm, emb_ref),
             ("tok", tok_hbm, tok_ref),
-            ("filt", filt_hbm.at[own, :], r_filt.at[a]),
             ("mix", mix_hbm, mix_ref),
-            ("gain", gain_hbm, gain_ref),
-            ("blk", blk_hbm, blk_ref),
             ("oblk", oblk_hbm, oblk_ref),
             ("c1", c1_hbm, c1_ref),
             ("turn", turn_hbm, turn_ref),
             ("dft", dft_hbm, dft_ref),
+            ("filt", filt_hbm.at[own, :], r_filt.at[a]),
         )
     ):
         loads[name] = pltpu.make_async_copy(src, dst, lsem.at[n])
@@ -168,18 +172,28 @@
 
     row128, lane128 = iota2(128, 128)
     p_lane = lane128 >> 4
-
     row16, lane16 = iota2(16, 128)
+
     spread = ones_at(((lane16 & 15) == row16) & (lane16 < 48)).astype(BF)
-    loads["emb"].wait()
-    loads["tok"].wait()
+    for name in ("emb", "gain", "blk"):
+        loads[name].wait()
+    gain_row = gain_ref[...]
+    gain_col = jnp.sum(jnp.where(row128 == lane128, gain_row, 0.0), axis=1, keepdims=True)
     emb_t = mm_tn(emb_ref[...], spread)
-    s_ss[...] = jnp.broadcast_to(jnp.sum(emb_t * emb_t, axis=0, keepdims=True), (8, 128))
-
-    loads["omix"].wait()
+    squares = jnp.broadcast_to(jnp.sum(emb_t * emb_t, axis=0, keepdims=True), (128, 128))
+    first = jnp.where(
+        (lane128 >= 48) & (lane128 < 64), pltpu.roll(squares, 48, 1), 0.0
+    )
+    for p in range(3):
+        block = blk_ref[:, p * 128 : (p + 1) * 128]
+        hi, lo = split(jnp.where(p_lane == p, emb_t * gain_col, 0.0))
+        first += mm_tn(block, hi) + mm_tn(block, lo)
+    s_tab[...] = first.reshape(NT, 8, 128)
+
     tile_m = ones_at((lane16 & 15) == row16).astype(BF)
     row, lane = iota2(256, 128)
     sel_row = ones_at(((row & 7) == (lane >> 4)) & ((row >> 4) == (lane & 15))).astype(BF)
+    loads["omix"].wait()
     wide = mm(sel_row, mm(omix_ref[...], tile_m).astype(BF))
     row, lane = iota2(256, 256)
     keep = ((row & 7) == ((lane >> 4) & 7)) & (((row >> 3) & 1) == (lane >> 7))
@@ -187,38 +201,23 @@
     loads["cot"].wait()
     cot2 = jnp.concatenate([cot_ref[:, :1024], cot_ref[:, 1024:]], axis=0)
     s_back[...] = mm(w_back[...], cot2).astype(BF).reshape(NT, 16, 1024)
+
+    loads["tok"].wait()
     pl.semaphore_wait(barrier, NC - 1 + NT - 1)
-    x_ss.start()
+    x_tab.start()
     x_tok.start()
     x_back.start()
-    x_filt.start()
-    r_ss[b] = s_ss[...]
+    x_filt.start(1, 4)
+    r_tab[b] = s_tab[b]
     r_tok[a] = tok_ref[...]
-
     r_back[b] = s_back[b]
 
     sel_p = ones_at(((row128 & 7) == p_lane) & ((row128 >> 3) == (lane128 & 15))).astype(BF)
-    loads["mix"].wait()
+    for name in ("mix", "oblk", "c1", "turn", "dft", "filt"):
+        loads[name].wait()
     for p in range(3):
         wide = mm(sel_p, mm(mix_ref[p * 128 : (p + 1) * 128, :], tile_m).astype(BF))
         r_mix[p] = jnp.where((row128 & 7) == p_lane, wide, 0.0).astype(BF)
-    for name in ("gain", "blk", "oblk", "c1", "turn", "dft", "filt"):
-        loads[name].wait()
-    gain_row = gain_ref[...]
-    gain_col = jnp.sum(jnp.where(row128 == lane128, gain_row, 0.0), axis=1, keepdims=True)
-
-    x_ss.recv()
-    total = jnp.sum(r_ss[...], axis=0)[0:1, :]
-    scal_row = lax.rsqrt(total * (1.0 / WIDTH) + EPS)
-    normed = emb_t * scal_row * gain_col
-    first = jnp.zeros((128, 128), F32)
-    for p in range(3):
-        first += mm_tn(
-            blk_ref[:, p * 128 : (p + 1) * 128], jnp.where(p_lane == p, normed, 0.0).astype(BF)
-        )
-    s_tab[...] = first.reshape(NT, 8, 128)
-    x_tab.start()
-    r_tab[b] = s_tab[b]
 
     row, lane = iota2(128, 256)
     sel_col = ones_at(((lane >> 4) * 8 + (lane & 7)) == row).astype(BF)
@@ -238,6 +237,11 @@
 
     x_tab.recv()
     pieces = r_tab[...].reshape(128, 128)
+    squares = jnp.sum(pieces, axis=0, keepdims=True) * 0.125
+    squares = jnp.where((lane128 >= 48) & (lane128 < 64), squares, 0.0)[:8]
+    squares = pltpu.roll(squares, 80, 1) + pltpu.roll(squares, 96, 1) + pltpu.roll(squares, 112, 1)
+    scal_row = lax.rsqrt(squares[0:1, :] * (1.0 / WIDTH) + EPS)
+    pieces = pieces * scal_row
     table = jnp.zeros((128, 128), F32)
     for p in range(3):
         table += mm_tn(r_mix[p], jnp.where(p_lane == p, pieces, 0.0).astype(BF))
@@ -249,17 +253,6 @@
         hot_h = hot[a, :, h * 1024 : (h + 1) * 1024]
         outer[h * 128 : (h + 1) * 128, :] = mm(outer_w, jnp.concatenate([hot_h, hot_h], axis=0))
         embedded[h * 128 : (h + 1) * 128, :] = mm_tn(emb_ref[...], hot_h).astype(BF)
-
-    x_back.recv()
-    gbranch[...] = mm(w_two[...], r_back[...].reshape(256, 1024))
-    for h in range(2):
-        for s in range(8):
-            part = slice(s * 128, (s + 1) * 128)
-            hrow = slice(h * 128, (h + 1) * 128)
-            grid_a[pl.ds(h * 8 + s, 128, stride=16), :] = gbranch[hrow, part] * outer[hrow, part]
-    s_gf[...] = grid_a[...].astype(BF).reshape(NC, 16, 16, 128)
-    x_gf.start()
-    r_gf[a] = s_gf[a]
 
     mine = gated_t[pl.ds(pl.multiple_of(a * 16, 16), 16), :][:, :16].astype(BF)
     for src in range(NC):
@@ -323,6 +316,18 @@
 
     groups(gated_spectrum)
 
+    x_filt.start(4, 8)
+    x_back.recv()
+    gbranch[...] = mm(w_two[...], r_back[...].reshape(256, 1024))
+    for h in range(2):
+        for s in range(8):
+            part = slice(s * 128, (s + 1) * 128)
+            hrow = slice(h * 128, (h + 1) * 128)
+            grid_a[pl.ds(h * 8 + s, 128, stride=16), :] = gbranch[hrow, part] * outer[hrow, part]
+    s_gf[...] = grid_a[...].astype(BF).reshape(NC, 16, 16, 128)
+    x_gf.start()
+    r_gf[a] = s_gf[a]
+
     x_filt.recv()
     for src in range(NC):
         for q in range(16):
@@ -354,6 +359,25 @@
 
     groups(grad_group)
     r_fg[a] = s_fg[a]
+
+    def gated_group(n):
+        even = spec_s[rows_of(n), :]
+        spectrum = spec_g[rows_of(n), :] * jnp.concatenate([even, even], axis=1)
+        for u, result in enumerate(inverse(spectrum, i1_ref[...])):
+            start = pl.multiple_of(n * 512 + u * 128, 128)
+            grid_b[pl.ds(start, 128), :] = result
+
+    groups(gated_group)
+    sums = jnp.zeros((16, 32), F32)
+    for src in range(NC):
+        vals = jnp.concatenate(
+            [grid_b[pl.ds(src * 16 + q, 16, stride=128), :] for q in range(16)], axis=1
+        ).astype(BF)
+        hot_s = hot[src]
+        sums += mm_nt(vals, jnp.concatenate([hot_s, hot_s], axis=0))
+    s_gg[...] = jnp.concatenate([sums, jnp.zeros((16, 96), F32)], axis=1)
+    x_gg.start()
+    r_gg[a] = s_gg[...]
 
     for n in range(4):
         x_fl(n).recv()
@@ -381,25 +405,6 @@
     x_out.start()
     r_out[b] = s_out[b]
 
-    def gated_group(n):
-        even = spec_s[rows_of(n), :]
-        spectrum = spec_g[rows_of(n), :] * jnp.concatenate([even, even], axis=1)
-        for u, result in enumerate(inverse(spectrum, i1_ref[...])):
-            start = pl.multiple_of(n * 512 + u * 128, 128)
-            grid_b[pl.ds(start, 128), :] = result
-
-    groups(gated_group)
-    sums = jnp.zeros((16, 32), F32)
-    for src in range(NC):
-        vals = jnp.concatenate(
-            [grid_b[pl.ds(src * 16 + q, 16, stride=128), :] for q in range(16)], axis=1
-        ).astype(BF)
-        hot_s = hot[src]
-        sums += mm_nt(vals, jnp.concatenate([hot_s, hot_s], axis=0))
-    s_gg[...] = jnp.concatenate([sums, jnp.zeros((16, 96), F32)], axis=1)
-    x_gg.start()
-    r_gg[a] = s_gg[...]
-
     x_gg.recv()
     x_seg.recv()
     seg = jnp.sum(r_seg[...], axis=0)
@@ -416,7 +421,7 @@
     for p in range(3):
         hi, lo = split(jnp.where(p_lane == p, grads, 0.0))
         gfirst += mm(r_mix[p], hi) + mm(r_mix[p], lo)
-    share = jnp.sum(gfirst * r_tab[...].reshape(128, 128), axis=0, keepdims=True) / scal_row
+    share = jnp.sum(gfirst * r_tab[...].reshape(128, 128), axis=0, keepdims=True)
     share = jnp.broadcast_to(share, (128, 128))
     share = pltpu.roll(share, 48, 1) + pltpu.roll(share, 32, 1) + pltpu.roll(share, 16, 1)
     s_gt[...] = jnp.where(
@@ -449,7 +454,7 @@
         x_fg(n).recv()
 
     for exchange in (
-        x_filt, x_tok, x_gf, x_gg, x_seg, x_back, x_ss, x_tab, x_out, x_gt,
+        x_filt, x_tok, x_gf, x_gg, x_seg, x_back, x_tab, x_out, x_gt,
         *[x_fl(n) for n in range(4)], *[x_fg(n) for n in range(4)],
     ):
         exchange.drain()
@@ -496,7 +501,6 @@
         V((16, 128), F32), V((NC, 16, 128), F32),
         V((2, 16, 128), F32), V((NC, 2, 16, 128), F32),
         V((NT, 16, 1024), BF), V((NT, 16, 1024), BF),
-        V((8, 128), F32), V((NT, 8, 128), F32),
         V((NT, 8, 128), F32), V((NT, 8, 128), F32),
         V((NT, 16, 1024), BF),
         V((NT, 8, 128), F32), V((NT, 8, 128), F32),
@@ -507,7 +511,7 @@
         V((2048, 256), F32), V((2048, 256), F32), V((2048, 128), F32),
         V((256, 1024), F32), V((256, 1024), F32),
         pltpu.SemaphoreType.DMA((13, NC)), pltpu.SemaphoreType.DMA((13, NC)),
-        pltpu.SemaphoreType.DMA((5, NT)), pltpu.SemaphoreType.DMA((5, NT)), pltpu.SemaphoreType.DMA((12,)),
+        pltpu.SemaphoreType.DMA((4, NT)), pltpu.SemaphoreType.DMA((4, NT)), pltpu.SemaphoreType.DMA((12,)),
     ]
     received = pl.pallas_call(
         kernel,

time: 70.7 us -> 62.3 us (0.88)
  Pallas kernels: 69.9 us -> 61.5 us
    pallas_call x1, Pallas kernels: 67.3 us -> 58.9 us  [local(): pl.pallas_call(kernel, out_shape=(jax.ShapeDtypeStruct((NT, 16, 1024), BF...]
where the time goes in v3:
time: 62.3 us; the launch traced here: 62.1 us
  Pallas kernels  61.5 us (99%)
  between operations  0.64 us (1%)
    pallas_call x1, Pallas kernels, local(): pl.pallas_call(kernel, out_shape=(jax.ShapeDtypeStruct((NT, 16, 1024), BF...  58.9 us
    pallas_call x1, Pallas kernels, local(): pl.pallas_call(finish, out_shape=(jax.ShapeDtypeStruct((128, 2048), BF),...  2.64 us

profile of v3, /device:TPU:1, one launch (start us, length us, event | category | flops | bytes accessed | tf_op | source)
XLA Modules:
  0.0 62.1 jit_solution(13782731340718331495)
XLA Ops:
  0.6 58.9 %shard_map.147 = (bf16[16,16,1024]{2,1,0:T(8,128)(2,1)}, bf16[8,16,16,128]{3,2,1,0:T(8,128)(2,1)}, bf16[256,256]{1,0:T(8,128)(2,1)}, bf16[256,1024]{1,0:T(8,128)(2,1)}, f32[24,128]{1,0:T(8,128)}) custom-call(s32[16,128]{1,0:T(8,128)} %bitcast.11, bf16[16,128]{1,0:T(8,128)(2,1)} %emb_hbm.1, f32[1,128]{1,0:T(1,128)} %bitcast.12, bf16[128,384]{1,0:T(8,128)(2,1)} %bitcast.7, ...), custom_call_target="tpu_custom_call" | custom-call | tf_op jit(solution)/shard_map/pallas_call | solution.py:516
  59.5 2.6 %shard_map.148 = (bf16[128,2048]{1,0:T(8,128)(2,1)}, f32[128,2048]{1,0:T(8,128)}, f32[16,128]{1,0:T(8,128)}, f32[1,128]{1,0:T(1,128)}) custom-call(bf16[16,16,1024]{2,1,0:T(8,128)(2,1)} %get-tuple-element.13.out_hbm, bf16[8,16,16,128]{3,2,1,0:T(8,128)(2,1)} %get-tuple-element.14.fg_hbm, bf16[256,256]{1,0:T(8,128)(2,1)} %get-tuple-element.15.w_hbm, ...), custom_call_target="tpu_custom_call" | custom-call | tf_op jit(solution)/shard_map/pallas_call | solution.py:543

commit v4 on v3

--- a/solution.py
+++ b/solution.py
@@ -15,7 +15,7 @@
 F32 = jnp.float32
 MESH = pl.DeviceIdType.MESH
 
-FILT_IN, TOK, GF, GG, SEG, FILT, FG = 0, 1, 2, 3, 4, 5, 9
+FILT_IN, TOK, GF, FIN, FILT, FG = 0, 1, 2, 3, 4, 8
 BACK, TAB, OUT, GT = range(4)
 
 
@@ -71,9 +71,9 @@
     c1_hbm, turn_hbm, dft_hbm,
     r_out, r_fg, w_back, embedded, small,
     tok_ref, emb_ref, gain_ref, blk_ref, mix_ref, oblk_ref, omix_ref, cot_ref, c1_ref, turn_ref, dft_ref,
-    r_filt, r_tok, s_gf, r_gf, s_fl, r_fl, s_fg, s_gg, r_gg, s_seg, r_seg,
+    r_filt, r_tok, s_gf, r_gf, s_fl, r_fl, s_fg, own_gg, s_fin, r_fin,
     s_back, r_back, s_tab, r_tab, s_out, s_gt, r_gt,
-    w_two, r_mix, hot, tall, gated_t, grid_a, grid_b, spec_x, spec_g, spec_s, outer, gbranch,
+    w_two, r_mix, hot, firsts, tall, gated_t, grid_a, grid_b, spec_x, spec_g, spec_s, outer, gbranch,
     ssem_c, rsem_c, ssem_t, rsem_t, lsem,
 ):
     a = lax.axis_index("ctx")
@@ -128,8 +128,7 @@
     quarter = lambda ref, n: (lambda p: ref.at[p, pl.ds(n * 4, 4)])
     x_fl = lambda n: Exchange("ctx", FILT + n, quarter(s_fl, n), quarter(r_fl, n))
     x_fg = lambda n: Exchange("ctx", FG + n, quarter(s_fg, n), quarter(r_fg, n))
-    x_gg = Exchange("ctx", GG, whole(s_gg), slot(r_gg))
-    x_seg = Exchange("ctx", SEG, whole(s_seg), slot(r_seg))
+    x_fin = Exchange("ctx", FIN, whole(s_fin), slot(r_fin))
     x_back = Exchange("tp", BACK, slot(s_back), slot(r_back))
     x_tab = Exchange("tp", TAB, slot(s_tab), slot(r_tab))
     x_out = Exchange("tp", OUT, slot(s_out), slot(r_out))
@@ -174,21 +173,21 @@
     p_lane = lane128 >> 4
     row16, lane16 = iota2(16, 128)
 
-    spread = ones_at(((lane16 & 15) == row16) & (lane16 < 48)).astype(BF)
+    eye = ones_at(row128 == lane128).astype(BF)
     for name in ("emb", "gain", "blk"):
         loads[name].wait()
     gain_row = gain_ref[...]
-    gain_col = jnp.sum(jnp.where(row128 == lane128, gain_row, 0.0), axis=1, keepdims=True)
-    emb_t = mm_tn(emb_ref[...], spread)
-    squares = jnp.broadcast_to(jnp.sum(emb_t * emb_t, axis=0, keepdims=True), (128, 128))
-    first = jnp.where(
-        (lane128 >= 48) & (lane128 < 64), pltpu.roll(squares, 48, 1), 0.0
-    )
-    for p in range(3):
-        block = blk_ref[:, p * 128 : (p + 1) * 128]
-        hi, lo = split(jnp.where(p_lane == p, emb_t * gain_col, 0.0))
-        first += mm_tn(block, hi) + mm_tn(block, lo)
-    s_tab[...] = first.reshape(NT, 8, 128)
+    hi = gain_row.astype(BF).astype(F32)
+    mid = (gain_row - hi).astype(BF).astype(F32)
+    row8 = lax.broadcasted_iota(jnp.int32, (8, 128), 0)
+    gains = jnp.where(row8 == 0, hi, jnp.where(row8 == 1, mid, gain_row - hi - mid))
+    gains = jnp.where(row8 < 3, gains, 0.0)
+    turned = [
+        mm_tn(blk_ref[:, p * 128 : (p + 1) * 128], eye).reshape(NT, 8, 128) for p in range(3)
+    ]
+    turned.append(jnp.broadcast_to(gains[None], (NT, 8, 128)))
+    s_tab[:, 0:32, :] = jnp.concatenate(turned, axis=1).astype(BF)
+    s_tab[:, 32:48, :] = jnp.broadcast_to(emb_ref[...][None], (NT, 16, 128))
 
     tile_m = ones_at((lane16 & 15) == row16).astype(BF)
     row, lane = iota2(256, 128)
@@ -207,7 +206,7 @@
     x_tab.start()
     x_tok.start()
     x_back.start()
-    x_filt.start(1, 4)
+    x_filt.start()
     r_tab[b] = s_tab[b]
     r_tok[a] = tok_ref[...]
     r_back[b] = s_back[b]
@@ -236,15 +235,28 @@
             ).astype(BF)
 
     x_tab.recv()
-    pieces = r_tab[...].reshape(128, 128)
-    squares = jnp.sum(pieces, axis=0, keepdims=True) * 0.125
-    squares = jnp.where((lane128 >= 48) & (lane128 < 64), squares, 0.0)[:8]
-    squares = pltpu.roll(squares, 80, 1) + pltpu.roll(squares, 96, 1) + pltpu.roll(squares, 112, 1)
-    scal_row = lax.rsqrt(squares[0:1, :] * (1.0 / WIDTH) + EPS)
-    pieces = pieces * scal_row
+    squares = jnp.zeros((16, 128), F32)
+    for g in range(NT):
+        part = r_tab[g, 32:48, :].astype(F32)
+        squares += part * part
+    scal_col = lax.rsqrt(jnp.sum(squares, axis=1, keepdims=True) * (1.0 / WIDTH) + EPS)
+    scal_row = jnp.sum(
+        jnp.where((lane16 & 15) == row16, scal_col, 0.0), axis=0, keepdims=True
+    )
+    pieces = []
+    for g in range(NT):
+        top = r_tab[g, 16:32, :].astype(F32)
+        gain_g = top[8:9, :] + top[9:10, :] + top[10:11, :]
+        normed = (r_tab[g, 32:48, :].astype(F32) * scal_col * gain_g).astype(BF)
+        pieces.append(mm_nt(r_tab[g, 0:32, :], jnp.concatenate([normed] * 8, axis=0)))
+    first = jnp.zeros((128, 128), F32)
+    for p in range(3):
+        part = jnp.concatenate([piece[p * 8 : (p + 1) * 8] for piece in pieces], axis=0)
+        first += jnp.where(p_lane == p, part, 0.0)
+    firsts[...] = first
     table = jnp.zeros((128, 128), F32)
     for p in range(3):
-        table += mm_tn(r_mix[p], jnp.where(p_lane == p, pieces, 0.0).astype(BF))
+        table += mm_tn(r_mix[p], jnp.where(p_lane == p, first, 0.0).astype(BF))
     tall[...] = table
     gated_t[...] = table * pltpu.roll(table, 112, 1)
     outer_hi, outer_lo = split(pltpu.roll(table, 96, 1)[:, :16])
@@ -316,7 +328,6 @@
 
     groups(gated_spectrum)
 
-    x_filt.start(4, 8)
     x_back.recv()
     gbranch[...] = mm(w_two[...], r_back[...].reshape(256, 1024))
     for h in range(2):
@@ -375,9 +386,8 @@
         ).astype(BF)
         hot_s = hot[src]
         sums += mm_nt(vals, jnp.concatenate([hot_s, hot_s], axis=0))
-    s_gg[...] = jnp.concatenate([sums, jnp.zeros((16, 96), F32)], axis=1)
-    x_gg.start()
-    r_gg[a] = s_gg[...]
+    own_gg[...] = jnp.zeros((128, 128), F32)
+    own_gg[own, :] = jnp.concatenate([sums, jnp.zeros((16, 96), F32)], axis=1)
 
     for n in range(4):
         x_fl(n).recv()
@@ -395,33 +405,21 @@
         hi, lo = split(gbranch[hrow, :] * filtered)
         gp2 += mm_nt(hot_h, hi) + mm_nt(hot_h, lo)
         ctt += mm_nt(hot_h, cot_ref[:, h * 1024 : (h + 1) * 1024])
-    s_seg[0] = gp2
-    s_seg[1] = ctt
-    x_seg.start()
-    r_seg[a] = s_seg[...]
-    s_out[...] = (
-        mm_tn(w_two[...], jnp.concatenate(branch, axis=0)).astype(BF).reshape(NT, 16, 1024)
-    )
-    x_out.start()
-    r_out[b] = s_out[b]
-
-    x_gg.recv()
-    x_seg.recv()
-    seg = jnp.sum(r_seg[...], axis=0)
-    ctt = seg[1]
-    hi, rest = seg[0].astype(BF), seg[0] - seg[0].astype(BF).astype(F32)
+
+    hi = gp2.astype(BF)
+    rest = gp2 - hi.astype(F32)
     mid, low_part = split(rest)
     row48, lane48 = iota2(48, 128)
     place = ones_at(((row48 & 15) + 32) == lane48).astype(BF)
     gp2_t = mm_tn(jnp.concatenate([hi, mid, low_part], axis=0), place)
     table = tall[...]
     swapped = jnp.where(lane128 < 16, pltpu.roll(table, 112, 1), pltpu.roll(table, 16, 1))
-    grads = jnp.where(lane128 < 32, r_gg[...].reshape(128, 128) * swapped, gp2_t)
+    grads = jnp.where(lane128 < 32, own_gg[...] * swapped, gp2_t)
     gfirst = jnp.zeros((128, 128), F32)
     for p in range(3):
         hi, lo = split(jnp.where(p_lane == p, grads, 0.0))
         gfirst += mm(r_mix[p], hi) + mm(r_mix[p], lo)
-    share = jnp.sum(gfirst * r_tab[...].reshape(128, 128), axis=0, keepdims=True)
+    share = jnp.sum(gfirst * firsts[...], axis=0, keepdims=True) / scal_row
     share = jnp.broadcast_to(share, (128, 128))
     share = pltpu.roll(share, 48, 1) + pltpu.roll(share, 32, 1) + pltpu.roll(share, 16, 1)
     s_gt[...] = jnp.where(
@@ -429,6 +427,12 @@
     ).reshape(NT, 8, 128)
     x_gt.start()
     r_gt[b] = s_gt[b]
+
+    s_out[...] = (
+        mm_tn(w_two[...], jnp.concatenate(branch, axis=0)).astype(BF).reshape(NT, 16, 1024)
+    )
+    x_out.start()
+    r_out[b] = s_out[b]
 
     x_gt.recv()
     gt = r_gt[...].reshape(128, 128).T
@@ -439,22 +443,25 @@
         gnt += mm_nt(hi, block) + mm_nt(lo, block)
     cross = jnp.sum(gt[48:64, :], axis=1, keepdims=True) * 0.125
     emb = emb_ref[...].astype(F32)
-    scal_col = jnp.sum(jnp.where(lane16 == row16, scal_row, 0.0), axis=1, keepdims=True)
-    small[16:24, :] = jnp.broadcast_to(
+    s_fin[16:24, :] = jnp.broadcast_to(
         jnp.sum(gnt * emb * scal_col, axis=0, keepdims=True), (8, 128)
     )
-    small[0:16, :] = (
+    s_fin[0:16, :] = (
         ctt
         + scal_col * gain_row * gnt
         - emb * (scal_col * scal_col * scal_col * cross * (1.0 / WIDTH))
     )
+    x_fin.start()
+    r_fin[a] = s_fin[...]
+    x_fin.recv()
+    small[...] = jnp.sum(r_fin[...], axis=0)
 
     x_out.recv()
     for n in range(4):
         x_fg(n).recv()
 
     for exchange in (
-        x_filt, x_tok, x_gf, x_gg, x_seg, x_back, x_tab, x_out, x_gt,
+        x_filt, x_tok, x_gf, x_fin, x_back, x_tab, x_out, x_gt,
         *[x_fl(n) for n in range(4)], *[x_fg(n) for n in range(4)],
     ):
         exchange.drain()
@@ -498,19 +505,18 @@
         V((NC, 16, 16, 128), BF), V((NC, 16, 16, 128), BF),
         V((NC, 16, 16, 128), BF), V((NC, 16, 16, 128), BF),
         V((NC, 16, 16, 128), BF),
-        V((16, 128), F32), V((NC, 16, 128), F32),
-        V((2, 16, 128), F32), V((NC, 2, 16, 128), F32),
+        V((128, 128), F32), V((24, 128), F32), V((NC, 24, 128), F32),
         V((NT, 16, 1024), BF), V((NT, 16, 1024), BF),
-        V((NT, 8, 128), F32), V((NT, 8, 128), F32),
+        V((NT, 48, 128), BF), V((NT, 48, 128), BF),
         V((NT, 16, 1024), BF),
         V((NT, 8, 128), F32), V((NT, 8, 128), F32),
         V((256, 256), BF), V((3, 128, 128), BF),
         V((NC, 16, 2048), BF),
-        V((128, 128), F32), V((128, 128), F32),
+        V((128, 128), F32), V((128, 128), F32), V((128, 128), F32),
         V((2048, 128), F32), V((2048, 128), F32),
         V((2048, 256), F32), V((2048, 256), F32), V((2048, 128), F32),
         V((256, 1024), F32), V((256, 1024), F32),
-        pltpu.SemaphoreType.DMA((13, NC)), pltpu.SemaphoreType.DMA((13, NC)),
+        pltpu.SemaphoreType.DMA((12, NC)), pltpu.SemaphoreType.DMA((12, NC)),
         pltpu.SemaphoreType.DMA((4, NT)), pltpu.SemaphoreType.DMA((4, NT)), pltpu.SemaphoreType.DMA((12,)),
     ]
     received = pl.pallas_call(

time: 62.3 us -> 58.4 us (0.937)
  Pallas kernels: 61.5 us -> 57.6 us
    pallas_call x1, Pallas kernels: 58.9 us -> 55 us  [local(): pl.pallas_call(kernel, out_shape=(jax.ShapeDtypeStruct((NT, 16, 1024), BF...]
where the time goes in v4:
time: 58.4 us; the launch traced here: 58.3 us
  Pallas kernels  57.6 us (99%)
  between operations  0.64 us (1%)
    pallas_call x1, Pallas kernels, local(): pl.pallas_call(kernel, out_shape=(jax.ShapeDtypeStruct((NT, 16, 1024), BF...  55 us
    pallas_call x1, Pallas kernels, local(): pl.pallas_call(finish, out_shape=(jax.ShapeDtypeStruct((128, 2048), BF),...  2.64 us

profile of v4, /device:TPU:1, one launch (start us, length us, event | category | flops | bytes accessed | tf_op | source)
XLA Modules:
  0.0 58.3 jit_solution(17111617688447759184)
XLA Ops:
  0.6 55.0 %shard_map.147 = (bf16[16,16,1024]{2,1,0:T(8,128)(2,1)}, bf16[8,16,16,128]{3,2,1,0:T(8,128)(2,1)}, bf16[256,256]{1,0:T(8,128)(2,1)}, bf16[256,1024]{1,0:T(8,128)(2,1)}, f32[24,128]{1,0:T(8,128)}) custom-call(s32[16,128]{1,0:T(8,128)} %bitcast.11, bf16[16,128]{1,0:T(8,128)(2,1)} %emb_hbm.1, f32[1,128]{1,0:T(1,128)} %bitcast.12, bf16[128,384]{1,0:T(8,128)(2,1)} %bitcast.7, ...), custom_call_target="tpu_custom_call" | custom-call | tf_op jit(solution)/shard_map/pallas_call | solution.py:522
  55.6 2.6 %shard_map.148 = (bf16[128,2048]{1,0:T(8,128)(2,1)}, f32[128,2048]{1,0:T(8,128)}, f32[16,128]{1,0:T(8,128)}, f32[1,128]{1,0:T(1,128)}) custom-call(bf16[16,16,1024]{2,1,0:T(8,128)(2,1)} %get-tuple-element.13.out_hbm, bf16[8,16,16,128]{3,2,1,0:T(8,128)(2,1)} %get-tuple-element.14.fg_hbm, bf16[256,256]{1,0:T(8,128)(2,1)} %get-tuple-element.15.w_hbm, ...), custom_call_target="tpu_custom_call" | custom-call | tf_op jit(solution)/shard_map/pallas_call | solution.py:549

commit v5 on v4

--- a/solution.py
+++ b/solution.py
@@ -69,9 +69,9 @@
 def kernel(
     tok_hbm, emb_hbm, gain_hbm, blk_hbm, mix_hbm, oblk_hbm, omix_hbm, filt_hbm, cot_hbm,
     c1_hbm, turn_hbm, dft_hbm,
-    r_out, r_fg, w_back, embedded, small,
+    r_out, fgrad, w_back, embedded, small,
     tok_ref, emb_ref, gain_ref, blk_ref, mix_ref, oblk_ref, omix_ref, cot_ref, c1_ref, turn_ref, dft_ref,
-    r_filt, r_tok, s_gf, r_gf, s_fl, r_fl, s_fg, own_gg, s_fin, r_fin,
+    r_filt, r_tok, s_gf, r_gf, s_fl, r_fl, s_fg, r_fg, own_gg, s_fin, r_fin,
     s_back, r_back, s_tab, r_tab, s_out, s_gt, r_gt,
     w_two, r_mix, hot, firsts, tall, gated_t, grid_a, grid_b, spec_x, spec_g, spec_s, outer, gbranch,
     ssem_c, rsem_c, ssem_t, rsem_t, lsem,
@@ -453,12 +453,14 @@
     )
     x_fin.start()
     r_fin[a] = s_fin[...]
+    for n in range(4):
+        x_fg(n).recv()
+    grid_a[...] = r_fg[...].reshape(2048, 128).astype(F32)
+    for q in range(16):
+        fgrad[:, q * 128 : (q + 1) * 128] = grid_a[pl.ds(q, 128, stride=16), :]
     x_fin.recv()
     small[...] = jnp.sum(r_fin[...], axis=0)
-
     x_out.recv()
-    for n in range(4):
-        x_fg(n).recv()
 
     for exchange in (
         x_filt, x_tok, x_gf, x_fin, x_back, x_tab, x_out, x_gt,
@@ -468,33 +470,28 @@
 
 
 def finish(
-    out_hbm, fg_hbm, w_hbm, emb_hbm, small_hbm,
-    lay_ref, fgrad_ref, egrad_ref, ggrad_ref,
-    out_ref, fg_ref, w_ref, emb_ref, small_ref, grid, sem,
+    out_ref, fgrad_ref, w_ref, emb_ref, small_ref,
+    lay_hbm, fgrad_hbm, egrad_ref, ggrad_ref,
+    lay, sem,
 ):
-    pairs = (
-        (fg_hbm, fg_ref), (out_hbm, out_ref), (w_hbm, w_ref), (emb_hbm, emb_ref),
-        (small_hbm, small_ref),
-    )
-    copies = [pltpu.make_async_copy(src, dst, sem.at[n]) for n, (src, dst) in enumerate(pairs)]
-    for copy in copies:
-        copy.start()
-    copies[0].wait()
-    grid[...] = fg_ref[...].reshape(2048, 128).astype(F32)
-    for q in range(16):
-        fgrad_ref[:, q * 128 : (q + 1) * 128] = grid[pl.ds(q, 128, stride=16), :]
-    for copy in copies[1:]:
-        copy.wait()
+    copies = [pltpu.make_async_copy(fgrad_ref, fgrad_hbm, sem.at[2])]
+    copies[0].start()
     mixture = mm_tn(w_ref[...], out_ref[...].reshape(256, 1024))
     for h in range(2):
         hrow = slice(h * 128, (h + 1) * 128)
-        lay_ref[:, h * 1024 : (h + 1) * 1024] = (emb_ref[hrow].astype(F32) + mixture[hrow]).astype(BF)
+        cols = slice(h * 1024, (h + 1) * 1024)
+        lay[:, cols] = (emb_ref[hrow].astype(F32) + mixture[hrow]).astype(BF)
+        copies.append(pltpu.make_async_copy(lay.at[:, cols], lay_hbm.at[:, cols], sem.at[h]))
+        copies[-1].start()
     egrad_ref[...] = small_ref[0:16, :]
     ggrad_ref[...] = small_ref[16:17, :]
+    for copy in copies:
+        copy.wait()
 
 
 def local(token_ids, embedding, norm_gain, proj_blocks, proj_mixers, out_blocks, out_mixers, filters, cotangent):
     vmem = pl.BlockSpec(memory_space=pltpu.VMEM)
+    hbm = pl.BlockSpec(memory_space=pltpu.HBM)
     V = pltpu.VMEM
     scratch = [
         V((16, 128), jnp.int32), V((16, 128), BF), V((1, 128), F32), V((128, 384), BF),
@@ -504,7 +501,7 @@
         V((NC, 16, 128), jnp.int32),
         V((NC, 16, 16, 128), BF), V((NC, 16, 16, 128), BF),
         V((NC, 16, 16, 128), BF), V((NC, 16, 16, 128), BF),
-        V((NC, 16, 16, 128), BF),
+        V((NC, 16, 16, 128), BF), V((NC, 16, 16, 128), BF),
         V((128, 128), F32), V((24, 128), F32), V((NC, 24, 128), F32),
         V((NT, 16, 1024), BF), V((NT, 16, 1024), BF),
         V((NT, 48, 128), BF), V((NT, 48, 128), BF),
@@ -519,22 +516,7 @@
         pltpu.SemaphoreType.DMA((12, NC)), pltpu.SemaphoreType.DMA((12, NC)),
         pltpu.SemaphoreType.DMA((4, NT)), pltpu.SemaphoreType.DMA((4, NT)), pltpu.SemaphoreType.DMA((12,)),
     ]
-    received = pl.pallas_call(
-        kernel,
-        out_shape=(
-            jax.ShapeDtypeStruct((NT, 16, 1024), BF),
-            jax.ShapeDtypeStruct((NC, 16, 16, 128), BF),
-            jax.ShapeDtypeStruct((256, 256), BF),
-            jax.ShapeDtypeStruct((256, 1024), BF),
-            jax.ShapeDtypeStruct((24, 128), F32),
-        ),
-        in_specs=[pl.BlockSpec(memory_space=pltpu.HBM)] * 12,
-        out_specs=(vmem,) * 5,
-        scratch_shapes=scratch,
-        compiler_params=pltpu.CompilerParams(
-            collective_id=0, has_side_effects=True, vmem_limit_bytes=56 * 1024 * 1024
-        ),
-    )(
+    operands = (
         token_ids.reshape(16, 128),
         embedding,
         norm_gain.reshape(1, 128),
@@ -546,6 +528,24 @@
         cotangent,
         *dft_tables(),
     )
+    received = pl.pallas_call(
+        kernel,
+        out_shape=(
+            jax.ShapeDtypeStruct((NT, 16, 1024), BF),
+            jax.ShapeDtypeStruct((128, 2048), F32),
+            jax.ShapeDtypeStruct((256, 256), BF),
+            jax.ShapeDtypeStruct((256, 1024), BF),
+            jax.ShapeDtypeStruct((24, 128), F32),
+        ),
+        in_specs=[hbm] * 12,
+        out_specs=(vmem,) * 5,
+        scratch_shapes=scratch,
+        compiler_params=pltpu.CompilerParams(
+            collective_id=0, has_side_effects=True, vmem_limit_bytes=40 * 1024 * 1024
+        ),
+    )(
+        *[pltpu.with_memory_space_constraint(x, pltpu.HBM) for x in operands]
+    )
     layer_out, filter_grad, embed_grad, gain_grad = pl.pallas_call(
         finish,
         out_shape=(
@@ -554,13 +554,12 @@
             jax.ShapeDtypeStruct((16, 128), F32),
             jax.ShapeDtypeStruct((1, 128), F32),
         ),
-        in_specs=[pl.BlockSpec(memory_space=pltpu.HBM)] * 5,
-        out_specs=(vmem,) * 4,
+        in_specs=[vmem] * 5,
+        out_specs=(hbm, hbm, vmem, vmem),
         scratch_shapes=[
-            V((NT, 16, 1024), BF), V((NC, 16, 16, 128), BF), V((256, 256), BF), V((256, 1024), BF),
-            V((24, 128), F32), V((2048, 128), F32), pltpu.SemaphoreType.DMA((5,)),
+            V((128, 2048), BF), pltpu.SemaphoreType.DMA((3,)),
         ],
-        compiler_params=pltpu.CompilerParams(vmem_limit_bytes=56 * 1024 * 1024),
+        compiler_params=pltpu.CompilerParams(vmem_limit_bytes=16 * 1024 * 1024),
     )(*received)
     return layer_out, filter_grad, embed_grad, gain_grad.reshape(128)
 

time: 58.4 us -> 56.1 us (0.961)
  Pallas kernels: 57.6 us -> 55.4 us
    pallas_call x1, Pallas kernels: 55 us -> 53.6 us  [local(): pl.pallas_call(kernel, out_shape=(jax.ShapeDtypeStruct((NT, 16, 1024), BF...]
    pallas_call x1, Pallas kernels: 2.64 us -> 1.79 us  [local(): pl.pallas_call(finish, out_shape=(jax.ShapeDtypeStruct((128, 2048), BF),...]
where the time goes in v5:
time: 56.1 us; the launch traced here: 56 us
  Pallas kernels  55.4 us (99%)
  between operations  0.64 us (1%)
    pallas_call x1, Pallas kernels, local(): pl.pallas_call(kernel, out_shape=(jax.ShapeDtypeStruct((NT, 16, 1024), BF...  53.6 us
    pallas_call x1, Pallas kernels, local(): pl.pallas_call(finish, out_shape=(jax.ShapeDtypeStruct((128, 2048), BF),...  1.79 us

profile of v5, /device:TPU:1, one launch (start us, length us, event | category | flops | bytes accessed | tf_op | source)
XLA Modules:
  0.0 56.0 jit_solution(5155929447733300331)
XLA Ops:
  0.6 53.6 %shard_map.147 = (bf16[16,16,1024]{2,1,0:T(8,128)(2,1)S(1)}, f32[128,2048]{1,0:T(8,128)S(1)}, bf16[256,256]{1,0:T(8,128)(2,1)S(1)}, bf16[256,1024]{1,0:T(8,128)(2,1)S(1)}, f32[24,128]{1,0:T(8,128)S(1)}) custom-call(s32[16,128]{1,0:T(8,128)} %bitcast.11, bf16[16,128]{1,0:T(8,128)(2,1)} %emb_hbm.1, f32[1,128]{1,0:T(1,128)} %bitcast.12, ...), custom_call_target="tpu_custom_call" | custom-call | tf_op jit(solution)/shard_map/pallas_call | solution.py:531
  54.2 1.8 %shard_map.148 = (bf16[128,2048]{1,0:T(8,128)(2,1)}, f32[128,2048]{1,0:T(8,128)}, f32[16,128]{1,0:T(8,128)}, f32[1,128]{1,0:T(1,128)}) custom-call(bf16[16,16,1024]{2,1,0:T(8,128)(2,1)S(1)} %get-tuple-element.13.out_ref, f32[128,2048]{1,0:T(8,128)S(1)} %get-tuple-element.14.fgrad_ref, bf16[256,256]{1,0:T(8,128)(2,1)S(1)} %get-tuple-element.15.w_ref, ...), custom_call_target="tpu_custom_call" | custom-call | tf_op jit(solution)/shard_map/pallas_call | solution.py:549

commit v6 on v5

--- a/solution.py
+++ b/solution.py
@@ -15,7 +15,7 @@
 F32 = jnp.float32
 MESH = pl.DeviceIdType.MESH
 
-FILT_IN, TOK, GF, FIN, FILT, FG = 0, 1, 2, 3, 4, 8
+FILT_IN, TOK, GF, FIN, FILT, FG = 0, 1, 2, 3, 4, 6
 BACK, TAB, OUT, GT = range(4)
 
 
@@ -125,7 +125,7 @@
     x_filt = Exchange("ctx", FILT_IN, rows16(filt_hbm), slot(r_filt))
     x_tok = Exchange("ctx", TOK, whole(tok_ref), slot(r_tok))
     x_gf = Exchange("ctx", GF, slot(s_gf), slot(r_gf))
-    quarter = lambda ref, n: (lambda p: ref.at[p, pl.ds(n * 4, 4)])
+    quarter = lambda ref, n: (lambda p: ref.at[p, pl.ds(n * 8, 8)])
     x_fl = lambda n: Exchange("ctx", FILT + n, quarter(s_fl, n), quarter(r_fl, n))
     x_fg = lambda n: Exchange("ctx", FG + n, quarter(s_fg, n), quarter(r_fg, n))
     x_fin = Exchange("ctx", FIN, whole(s_fin), slot(r_fin))
@@ -189,6 +189,13 @@
     s_tab[:, 0:32, :] = jnp.concatenate(turned, axis=1).astype(BF)
     s_tab[:, 32:48, :] = jnp.broadcast_to(emb_ref[...][None], (NT, 16, 128))
 
+    loads["tok"].wait()
+    pl.semaphore_wait(barrier, NC - 1 + NT - 1)
+    x_tab.start()
+    x_tok.start()
+    r_tab[b] = s_tab[b]
+    r_tok[a] = tok_ref[...]
+
     tile_m = ones_at((lane16 & 15) == row16).astype(BF)
     row, lane = iota2(256, 128)
     sel_row = ones_at(((row & 7) == (lane >> 4)) & ((row >> 4) == (lane & 15))).astype(BF)
@@ -200,15 +207,8 @@
     loads["cot"].wait()
     cot2 = jnp.concatenate([cot_ref[:, :1024], cot_ref[:, 1024:]], axis=0)
     s_back[...] = mm(w_back[...], cot2).astype(BF).reshape(NT, 16, 1024)
-
-    loads["tok"].wait()
-    pl.semaphore_wait(barrier, NC - 1 + NT - 1)
-    x_tab.start()
-    x_tok.start()
     x_back.start()
     x_filt.start()
-    r_tab[b] = s_tab[b]
-    r_tok[a] = tok_ref[...]
     r_back[b] = s_back[b]
 
     sel_p = ones_at(((row128 & 7) == p_lane) & ((row128 >> 3) == (lane128 & 15))).astype(BF)
@@ -310,18 +310,15 @@
         return results
 
     def groups(body):
-        def step(n, carry):
+        for n in range(2):
             body(n)
-            return carry
-
-        lax.fori_loop(0, 4, step, 0)
 
     def rows_of(n):
-        return pl.ds(pl.multiple_of(n * 512, 512), 512)
+        return pl.ds(pl.multiple_of(n * 1024, 1024), 1024)
 
     def signals(ref, n):
         block = ref[rows_of(n), :].astype(BF)
-        return [block[u * 128 : (u + 1) * 128] for u in range(4)]
+        return [block[u * 128 : (u + 1) * 128] for u in range(8)]
 
     def gated_spectrum(n):
         spec_x[rows_of(n), :] = forward(signals(grid_a, n), c2_ref[...])
@@ -351,7 +348,7 @@
         spec_s[rows_of(n), :] = even
         spectrum = spec_x[rows_of(n), :] * jnp.concatenate([even, even], axis=1)
         for u, result in enumerate(inverse(spectrum, i1_ref[...])):
-            s_fl[:, n * 4 + u] = result.astype(BF).reshape(NC, 16, 128)
+            s_fl[:, n * 8 + u] = result.astype(BF).reshape(NC, 16, 128)
         x_fl(n).start()
 
     groups(filtered_group)
@@ -360,12 +357,12 @@
     x_gf.recv()
 
     def grad_group(n):
-        spectrum = forward([r_gf[:, n * 4 + u].reshape(128, 128) for u in range(4)], c2_ref[...])
+        spectrum = forward([r_gf[:, n * 8 + u].reshape(128, 128) for u in range(8)], c2_ref[...])
         spec_g[rows_of(n), :] = spectrum
         prod = spectrum * spec_x[rows_of(n), :]
         cross = 2.0 * (prod[:, :128] + prod[:, 128:])
         for u, result in enumerate(inverse(cross, i1_ref[:128, :])):
-            s_fg[:, n * 4 + u] = result.astype(BF).reshape(NC, 16, 128)
+            s_fg[:, n * 8 + u] = result.astype(BF).reshape(NC, 16, 128)
         x_fg(n).start()
 
     groups(grad_group)
@@ -375,7 +372,7 @@
         even = spec_s[rows_of(n), :]
         spectrum = spec_g[rows_of(n), :] * jnp.concatenate([even, even], axis=1)
         for u, result in enumerate(inverse(spectrum, i1_ref[...])):
-            start = pl.multiple_of(n * 512 + u * 128, 128)
+            start = pl.multiple_of(n * 1024 + u * 128, 128)
             grid_b[pl.ds(start, 128), :] = result
 
     groups(gated_group)
@@ -389,11 +386,22 @@
     own_gg[...] = jnp.zeros((128, 128), F32)
     own_gg[own, :] = jnp.concatenate([sums, jnp.zeros((16, 96), F32)], axis=1)
 
-    for n in range(4):
+    table = tall[...]
+    swapped = jnp.where(lane128 < 16, pltpu.roll(table, 112, 1), pltpu.roll(table, 16, 1))
+    grads = own_gg[...] * swapped
+    early = jnp.zeros((128, 128), F32)
+    for p in range(2):
+        hi, lo = split(jnp.where(p_lane == p, grads, 0.0))
+        early += mm(r_mix[p], hi) + mm(r_mix[p], lo)
+    ctt = jnp.zeros((16, 128), F32)
+    for h in range(2):
+        cols = slice(h * 1024, (h + 1) * 1024)
+        ctt += mm_nt(hot[a, :, cols], cot_ref[:, cols])
+
+    for n in range(2):
         x_fl(n).recv()
     grid_a[...] = r_fl[...].reshape(2048, 128).astype(F32)
     gp2 = jnp.zeros((16, 128), F32)
-    ctt = jnp.zeros((16, 128), F32)
     branch = []
     for h in range(2):
         hrow = slice(h * 128, (h + 1) * 128)
@@ -404,7 +412,6 @@
         hot_h = hot[a, :, h * 1024 : (h + 1) * 1024]
         hi, lo = split(gbranch[hrow, :] * filtered)
         gp2 += mm_nt(hot_h, hi) + mm_nt(hot_h, lo)
-        ctt += mm_nt(hot_h, cot_ref[:, h * 1024 : (h + 1) * 1024])
 
     hi = gp2.astype(BF)
     rest = gp2 - hi.astype(F32)
@@ -412,13 +419,8 @@
     row48, lane48 = iota2(48, 128)
     place = ones_at(((row48 & 15) + 32) == lane48).astype(BF)
     gp2_t = mm_tn(jnp.concatenate([hi, mid, low_part], axis=0), place)
-    table = tall[...]
-    swapped = jnp.where(lane128 < 16, pltpu.roll(table, 112, 1), pltpu.roll(table, 16, 1))
-    grads = jnp.where(lane128 < 32, own_gg[...] * swapped, gp2_t)
-    gfirst = jnp.zeros((128, 128), F32)
-    for p in range(3):
-        hi, lo = split(jnp.where(p_lane == p, grads, 0.0))
-        gfirst += mm(r_mix[p], hi) + mm(r_mix[p], lo)
+    hi, lo = split(gp2_t)
+    gfirst = early + mm(r_mix[2], hi) + mm(r_mix[2], lo)
     share = jnp.sum(gfirst * firsts[...], axis=0, keepdims=True) / scal_row
     share = jnp.broadcast_to(share, (128, 128))
     share = pltpu.roll(share, 48, 1) + pltpu.roll(share, 32, 1) + pltpu.roll(share, 16, 1)
@@ -453,7 +455,7 @@
     )
     x_fin.start()
     r_fin[a] = s_fin[...]
-    for n in range(4):
+    for n in range(2):
         x_fg(n).recv()
     grid_a[...] = r_fg[...].reshape(2048, 128).astype(F32)
     for q in range(16):
@@ -464,7 +466,7 @@
 
     for exchange in (
         x_filt, x_tok, x_gf, x_fin, x_back, x_tab, x_out, x_gt,
-        *[x_fl(n) for n in range(4)], *[x_fg(n) for n in range(4)],
+        *[x_fl(n) for n in range(2)], *[x_fg(n) for n in range(2)],
     ):
         exchange.drain()
 
@@ -513,7 +515,7 @@
         V((2048, 128), F32), V((2048, 128), F32),
         V((2048, 256), F32), V((2048, 256), F32), V((2048, 128), F32),
         V((256, 1024), F32), V((256, 1024), F32),
-        pltpu.SemaphoreType.DMA((12, NC)), pltpu.SemaphoreType.DMA((12, NC)),
+        pltpu.SemaphoreType.DMA((8, NC)), pltpu.SemaphoreType.DMA((8, NC)),
         pltpu.SemaphoreType.DMA((4, NT)), pltpu.SemaphoreType.DMA((4, NT)), pltpu.SemaphoreType.DMA((12,)),
     ]
     operands = (

time: 56.1 us -> 55.2 us (0.984)
  Pallas kernels: 55.4 us -> 54.3 us
    pallas_call x1, Pallas kernels: 53.6 us -> 52.5 us  [local(): pl.pallas_call(kernel, out_shape=(jax.ShapeDtypeStruct((NT, 16, 1024), BF...]
where the time goes in v6:
time: 55.2 us; the launch traced here: 55 us
  Pallas kernels  54.3 us (98%)
  between operations  0.64 us (1%)
    pallas_call x1, Pallas kernels, local(): pl.pallas_call(kernel, out_shape=(jax.ShapeDtypeStruct((NT, 16, 1024), BF...  52.5 us
    pallas_call x1, Pallas kernels, local(): pl.pallas_call(finish, out_shape=(jax.ShapeDtypeStruct((128, 2048), BF),...  1.79 us

profile of v6, /device:TPU:1, one launch (start us, length us, event | category | flops | bytes accessed | tf_op | source)
XLA Modules:
  0.0 55.0 jit_solution(5043033413975710655)
XLA Ops:
  0.6 52.5 %shard_map.147 = (bf16[16,16,1024]{2,1,0:T(8,128)(2,1)S(1)}, f32[128,2048]{1,0:T(8,128)S(1)}, bf16[256,256]{1,0:T(8,128)(2,1)S(1)}, bf16[256,1024]{1,0:T(8,128)(2,1)S(1)}, f32[24,128]{1,0:T(8,128)S(1)}) custom-call(s32[16,128]{1,0:T(8,128)} %bitcast.11, bf16[16,128]{1,0:T(8,128)(2,1)} %emb_hbm.1, f32[1,128]{1,0:T(1,128)} %bitcast.12, ...), custom_call_target="tpu_custom_call" | custom-call | tf_op jit(solution)/shard_map/pallas_call | solution.py:533
  53.2 1.8 %shard_map.148 = (bf16[128,2048]{1,0:T(8,128)(2,1)}, f32[128,2048]{1,0:T(8,128)}, f32[16,128]{1,0:T(8,128)}, f32[1,128]{1,0:T(1,128)}) custom-call(bf16[16,16,1024]{2,1,0:T(8,128)(2,1)S(1)} %get-tuple-element.13.out_ref, f32[128,2048]{1,0:T(8,128)S(1)} %get-tuple-element.14.fgrad_ref, bf16[256,256]{1,0:T(8,128)(2,1)S(1)} %get-tuple-element.15.w_ref, ...), custom_call_target="tpu_custom_call" | custom-call | tf_op jit(solution)/shard_map/pallas_call | solution.py:551

commit v7 on v6

--- a/solution.py
+++ b/solution.py
@@ -73,7 +73,7 @@
     tok_ref, emb_ref, gain_ref, blk_ref, mix_ref, oblk_ref, omix_ref, cot_ref, c1_ref, turn_ref, dft_ref,
     r_filt, r_tok, s_gf, r_gf, s_fl, r_fl, s_fg, r_fg, own_gg, s_fin, r_fin,
     s_back, r_back, s_tab, r_tab, s_out, s_gt, r_gt,
-    w_two, r_mix, hot, firsts, tall, gated_t, grid_a, grid_b, spec_x, spec_g, spec_s, outer, gbranch,
+    w_two, r_mix, hot, firsts, tall, gated_t, grid_a, grid_b, spec_x, spec_s, outer, gbranch,
     ssem_c, rsem_c, ssem_t, rsem_t, lsem,
 ):
     a = lax.axis_index("ctx")
@@ -336,6 +336,11 @@
     x_gf.start()
     r_gf[a] = s_gf[a]
 
+    ctt = jnp.zeros((16, 128), F32)
+    for h in range(2):
+        cols = slice(h * 1024, (h + 1) * 1024)
+        ctt += mm_nt(hot[a, :, cols], cot_ref[:, cols])
+
     x_filt.recv()
     for src in range(NC):
         for q in range(16):
@@ -358,24 +363,20 @@
 
     def grad_group(n):
         spectrum = forward([r_gf[:, n * 8 + u].reshape(128, 128) for u in range(8)], c2_ref[...])
-        spec_g[rows_of(n), :] = spectrum
         prod = spectrum * spec_x[rows_of(n), :]
         cross = 2.0 * (prod[:, :128] + prod[:, 128:])
         for u, result in enumerate(inverse(cross, i1_ref[:128, :])):
             s_fg[:, n * 8 + u] = result.astype(BF).reshape(NC, 16, 128)
         x_fg(n).start()
-
-    groups(grad_group)
-    r_fg[a] = s_fg[a]
-
-    def gated_group(n):
         even = spec_s[rows_of(n), :]
-        spectrum = spec_g[rows_of(n), :] * jnp.concatenate([even, even], axis=1)
+        spectrum = spectrum * jnp.concatenate([even, even], axis=1)
         for u, result in enumerate(inverse(spectrum, i1_ref[...])):
             start = pl.multiple_of(n * 1024 + u * 128, 128)
             grid_b[pl.ds(start, 128), :] = result
 
-    groups(gated_group)
+    groups(grad_group)
+    r_fg[a] = s_fg[a]
+
     sums = jnp.zeros((16, 32), F32)
     for src in range(NC):
         vals = jnp.concatenate(
@@ -393,10 +394,6 @@
     for p in range(2):
         hi, lo = split(jnp.where(p_lane == p, grads, 0.0))
         early += mm(r_mix[p], hi) + mm(r_mix[p], lo)
-    ctt = jnp.zeros((16, 128), F32)
-    for h in range(2):
-        cols = slice(h * 1024, (h + 1) * 1024)
-        ctt += mm_nt(hot[a, :, cols], cot_ref[:, cols])
 
     for n in range(2):
         x_fl(n).recv()
@@ -513,7 +510,7 @@
         V((NC, 16, 2048), BF),
         V((128, 128), F32), V((128, 128), F32), V((128, 128), F32),
         V((2048, 128), F32), V((2048, 128), F32),
-        V((2048, 256), F32), V((2048, 256), F32), V((2048, 128), F32),
+        V((2048, 256), F32), V((2048, 128), F32),
         V((256, 1024), F32), V((256, 1024), F32),
         pltpu.SemaphoreType.DMA((8, NC)), pltpu.SemaphoreType.DMA((8, NC)),
         pltpu.SemaphoreType.DMA((4, NT)), pltpu.SemaphoreType.DMA((4, NT)), pltpu.SemaphoreType.DMA((12,)),

time: 55.2 us -> 55.2 us (level)
  no operation moved by 1% of the time
where the time goes in v7:
time: 55.2 us; the launch traced here: 55 us
  Pallas kernels  54.3 us (98%)
  between operations  0.64 us (1%)
    pallas_call x1, Pallas kernels, local(): pl.pallas_call(kernel, out_shape=(jax.ShapeDtypeStruct((NT, 16, 1024), BF...  52.5 us
    pallas_call x1, Pallas kernels, local(): pl.pallas_call(finish, out_shape=(jax.ShapeDtypeStruct((128, 2048), BF),...  1.79 us

profile of v7, /device:TPU:1, one launch (start us, length us, event | category | flops | bytes accessed | tf_op | source)
XLA Modules:
  0.0 55.0 jit_solution(17140205843475168145)
XLA Ops:
  0.6 52.5 %shard_map.147 = (bf16[16,16,1024]{2,1,0:T(8,128)(2,1)S(1)}, f32[128,2048]{1,0:T(8,128)S(1)}, bf16[256,256]{1,0:T(8,128)(2,1)S(1)}, bf16[256,1024]{1,0:T(8,128)(2,1)S(1)}, f32[24,128]{1,0:T(8,128)S(1)}) custom-call(s32[16,128]{1,0:T(8,128)} %bitcast.11, bf16[16,128]{1,0:T(8,128)(2,1)} %emb_hbm.1, f32[1,128]{1,0:T(1,128)} %bitcast.12, ...), custom_call_target="tpu_custom_call" | custom-call | tf_op jit(solution)/shard_map/pallas_call | solution.py:530
  53.2 1.8 %shard_map.148 = (bf16[128,2048]{1,0:T(8,128)(2,1)}, f32[128,2048]{1,0:T(8,128)}, f32[16,128]{1,0:T(8,128)}, f32[1,128]{1,0:T(1,128)}) custom-call(bf16[16,16,1024]{2,1,0:T(8,128)(2,1)S(1)} %get-tuple-element.13.out_ref, f32[128,2048]{1,0:T(8,128)S(1)} %get-tuple-element.14.fgrad_ref, bf16[256,256]{1,0:T(8,128)(2,1)S(1)} %get-tuple-element.15.w_ref, ...), custom_call_target="tpu_custom_call" | custom-call | tf_op jit(solution)/shard_map/pallas_call | solution.py:548
